TPU v7x, 32 devices: a whole 2x2x4 slice. The times are simulated.
32 devices in a mesh: seq: 8 (over y, x, core), fsdp: 4 (over z).
Axes of the slice: x: 2, y: 2, z: 4, core: 2. Of those that a mesh axis runs over, the one named last changes fastest.
Arguments:
- inputs: bfloat16 [4, 4096, 1280], P('fsdp', 'seq'), may hold values from -6 to 6
- w_query: float32 [1280, 1280], P(('seq', 'fsdp')), may hold values from -0.15625 to 0.15625
- w_key: float32 [1280, 1280], P(('seq', 'fsdp')), may hold values from -0.15625 to 0.15625
- w_value: float32 [1280, 1280], P(('seq', 'fsdp')), may hold values from -0.15625 to 0.15625
- w_proj: float32 [1280, 1280], P(('seq', 'fsdp')), may hold values from -1 to 1
- w_up: float32 [1280, 1280], P(('seq', 'fsdp')), may hold values from -0.15625 to 0.15625
- w_down: float32 [1280, 1280], P(('seq', 'fsdp')), may hold values from -0.3125 to 0.3125
- gain_first: float32 [1280], P(('seq', 'fsdp')), may hold values from 0.25 to 1.75
- gain_second: float32 [1280], P(('seq', 'fsdp')), may hold values from 0.25 to 1.75
- bias_up: float32 [1280], P(('seq', 'fsdp')), may hold values from -3 to 3
- bias_down: float32 [1280], P(('seq', 'fsdp')), may hold values from -3 to 3
- query_scale: float32 [80], replicated, may hold values from 0 to 2
- cotangent: bfloat16 [4, 4096, 1280], P('fsdp', 'seq'), may hold values from -6 to 6
Outputs:
- result: bfloat16 [4, 4096, 1280], P('fsdp', 'seq')
- grad_inputs: bfloat16 [4, 4096, 1280], P('fsdp', 'seq')
- grad_query: float32 [1280, 1280], P(('seq', 'fsdp'))
- grad_key: float32 [1280, 1280], P(('seq', 'fsdp'))
- grad_value: float32 [1280, 1280], P(('seq', 'fsdp'))
- grad_proj: float32 [1280, 1280], P(('seq', 'fsdp'))
- grad_up: float32 [1280, 1280], P(('seq', 'fsdp'))
- grad_down: float32 [1280, 1280], P(('seq', 'fsdp'))
- grad_first: float32 [1280], P(('seq', 'fsdp'))
- grad_second: float32 [1280], P(('seq', 'fsdp'))
- grad_bias_up: float32 [1280], P(('seq', 'fsdp'))
- grad_bias_down: float32 [1280], P(('seq', 'fsdp'))
- grad_scale: float32 [80], replicated
All inputs are finite; a program needn't handle non-finite values.
Results may differ from a plain program's by a relative error of at most 0.015.
The roundings to bfloat16 on the way count: a program that leaves them out, or rounds other values in their place, can miss the bound.
Values may be sent and summed in bfloat16 or wider, within the bound.
A program may use at most 192 MiB of HBM per device.

v0:
```python
import functools
import math

import jax
import jax.numpy as jnp
from jax import lax
from jax.experimental import pallas as pl
from jax.experimental.pallas import tpu as pltpu
from jax.sharding import PartitionSpec as P

H = 16
HD = 80
eps_norm = 1e-06
log_two_inverse = 1.442695
bf = jnp.bfloat16
f32 = jnp.float32
NEG = -1e30


def dot(a,b,ca=1,cb=0):
    return lax.dot_general(a,b,(((ca,),(cb,)),((),())),preferred_element_type=f32)


MESH = pl.DeviceIdType.MESH


def spots():
    s, f = lax.axis_index("seq"), lax.axis_index("fsdp")
    return s, f, s // 2, lax.rem(s, 2)


def greet(S, F):
    s, f, _, _ = spots()
    barrier = pltpu.get_barrier_semaphore()
    for i in range(1, S):
        pl.semaphore_signal(barrier, inc=1, device_id=(lax.rem(s + i, S), f), device_id_type=MESH)
    for i in range(1, F):
        pl.semaphore_signal(barrier, inc=1, device_id=(s, lax.rem(f + i, F)), device_id_type=MESH)
    pl.semaphore_wait(barrier, S + F - 2)


def remote(src, dst, sends, recvs, n, to):
    return pltpu.make_async_remote_copy(
        src_ref=src,
        dst_ref=dst,
        send_sem=sends.at[n],
        recv_sem=recvs.at[n],
        device_id=to,
        device_id_type=MESH,
    )


def gather_kernel(S, F, x, wq, sm, wm, x_all, wq_all, sm_all, wm_all, xv, qv, sv, mv, local,
                  xs, xr, qs, qr, ss, sr, ms, mr):
    s, f, p, c = spots()
    P_ = S // 2
    other = 1 - c
    loads = [
        pltpu.make_async_copy(sm, sv, local.at[0]),
        pltpu.make_async_copy(wq, qv, local.at[1]),
        pltpu.make_async_copy(x, xv, local.at[2]),
        pltpu.make_async_copy(wm, mv, local.at[3]),
    ]
    for load in loads:
        load.start()
    greet(S, F)
    mate = (p * 2 + other, f)
    todo = []

    def go(copy):
        copy.start()
        todo.append(copy)

    def chip(i):
        return lax.rem(p + i, P_) * 2 + c

    def back(i):
        return lax.rem(p + P_ - i, P_) * 2 + c

    def near_chip(i):
        return flip_bits(p, i) * 2 + c

    H_ = x.shape[0] // 2

    def deep(i):
        return lax.rem(f + i, F)

    def behind(i):
        return lax.rem(f + F - i, F)

    loads[0].wait()
    keep0 = pltpu.make_async_copy(sv, sm_all.at[s, f], local.at[0])
    keep0.start()
    for i in range(1, F):
        go(remote(sv, sm_all.at[s, f], ss, sr, i, (s, deep(i))))
    loads[1].wait()
    keep1 = pltpu.make_async_copy(qv.at[s], wq_all.at[s, f], local.at[1])
    keep1.start()
    for i in range(1, S):
        to = lax.rem(s + i, S)
        go(remote(qv.at[to], wq_all.at[s, f], qs, qr, i, (to, f)))
    loads[2].wait()
    keep2 = pltpu.make_async_copy(xv, x_all.at[s], local.at[2])
    keep2.start()
    if P_ == 4:
        for first in range(2):
            for i in (1, 2):
                half = first if i == 1 else 1 - first
                part = pl.ds(half * H_, H_)
                go(remote(xv.at[part], x_all.at[s, part], xs, xr, 2 * i + half, (near_chip(i), f)))
    else:
        for i in range(1, P_):
            go(remote(xv, x_all.at[s], xs, xr, i, (chip(i), f)))
    go(remote(xv, x_all.at[s], xs, xr, 0, mate))
    loads[3].wait()
    keep3 = pltpu.make_async_copy(mv, wm_all.at[:, f], local.at[3])
    keep3.start()
    for i in range(1, F):
        go(remote(mv, wm_all.at[:, f], ms, mr, i, (s, deep(i))))
    for i in range(1, F):
        g = behind(i)
        remote(sv, sm_all.at[s, g], ss, sr, i, mate).wait_recv()
    keep0.wait()
    for i in range(1, S):
        go(remote(sm_all.at[s], sm_all.at[s], ss, sr, F - 1 + i, (lax.rem(s + i, S), f)))
    for i in range(1, S):
        remote(qv.at[0], wq_all.at[lax.rem(s + S - i, S), f], qs, qr, i, mate).wait_recv()
    keep1.wait()
    for i in range(1, F):
        go(remote(wq_all.at[:, f], wq_all.at[:, f], qs, qr, S - 1 + i, (s, deep(i))))
    for i in range(1, F):
        remote(mv, wm_all.at[:, behind(i)], ms, mr, i, mate).wait_recv()
    keep3.wait()
    if P_ == 4:
        for i in (1, 2):
            half = i - 1
            part = pl.ds(half * H_, H_)
            src = near_chip(i)
            remote(xv.at[part], x_all.at[src, part], xs, xr, 2 * i + half, mate).wait_recv()
            blk = x_all.at[src, part]
            go(remote(blk, blk, xs, xr, 6 + half, (near_chip(3 - i), f)))
        for i in (1, 2):
            half = 2 - i
            part = pl.ds(half * H_, H_)
            src = near_chip(i)
            remote(xv.at[part], x_all.at[src, part], xs, xr, 2 * i + half, mate).wait_recv()
            go(remote(x_all.at[src], x_all.at[src], xs, xr, 8 + i, mate))
    for i in range(1, P_ if P_ != 4 else 1):
        src = back(i)
        remote(xv, x_all.at[src], xs, xr, i, mate).wait_recv()
        go(remote(x_all.at[src], x_all.at[src], xs, xr, P_ - 1 + i, mate))
    for i in range(1, S):
        src = lax.rem(s + S - i, S)
        remote(sm_all.at[src], sm_all.at[src], ss, sr, F - 1 + i, mate).wait_recv()
    for i in range(1, F):
        g = behind(i)
        remote(wq_all.at[:, g], wq_all.at[:, g], qs, qr, S - 1 + i, mate).wait_recv()
    near = p * 2 + other
    remote(xv, x_all.at[near], xs, xr, 0, mate).wait_recv()
    if P_ == 4:
        for half in range(2):
            part = pl.ds(half * H_, H_)
            blk = x_all.at[near_chip(3), part]
            remote(blk, blk, xs, xr, 6 + half, mate).wait_recv()
            go(remote(blk, blk, xs, xr, 11 + half, mate))
        for i in (1, 2):
            blk = x_all.at[flip_bits(p, i) * 2 + other]
            remote(blk, blk, xs, xr, 8 + i, mate).wait_recv()
        for half in range(2):
            blk = x_all.at[flip_bits(p, 3) * 2 + other, pl.ds(half * H_, H_)]
            remote(blk, blk, xs, xr, 11 + half, mate).wait_recv()
    else:
        for i in range(1, P_):
            src = lax.rem(p + P_ - i, P_) * 2 + other
            remote(xv, x_all.at[src], xs, xr, P_ - 1 + i, mate).wait_recv()
    keep2.wait()
    for copy in todo:
        copy.wait_send()


def gather_all(S, F, x, wq, sm, wm):
    any_ = pl.BlockSpec(memory_space=pl.ANY)
    shapes = [
        (S,) + x.shape,
        (S, F) + wq.shape[1:],
        (S, F) + sm.shape,
        (wm.shape[0], F) + wm.shape[1:],
    ]
    P_ = S // 2
    dma = pltpu.SemaphoreType.DMA
    counts = [max(2 * P_ - 1, 12), S + F - 1, F + S - 1, F]
    sems = []
    for n in counts:
        sems += [dma((n + 1,)), dma((n + 1,))]
    return pl.pallas_call(
        functools.partial(gather_kernel, S, F),
        out_shape=[
            jax.ShapeDtypeStruct(sh, a.dtype) for sh, a in zip(shapes, (x, wq, sm, wm), strict=True)
        ],
        in_specs=[any_] * 4,
        out_specs=[any_] * 4,
        scratch_shapes=[
            pltpu.VMEM(x.shape, x.dtype),
            pltpu.VMEM(wq.shape, wq.dtype),
            pltpu.VMEM(sm.shape, sm.dtype),
            pltpu.VMEM(wm.shape, wm.dtype),
            dma((4,)),
        ]
        + sems,
        compiler_params=pltpu.CompilerParams(collective_id=1, has_side_effects=True),
        name="gather",
    )(x, wq, sm, wm)


def xor(a, b, n):
    out, bit = 0, 1
    while bit < n:
        both = lax.rem(lax.div(a, bit), 2) + lax.rem(lax.div(b, bit), 2)
        out = out + bit * lax.rem(both, 2)
        bit *= 2
    return out


def flip_bits(p, i):
    out, bit = p, 1
    while bit <= i:
        if i & bit:
            out = out + bit - 2 * bit * lax.rem(lax.div(p, bit), 2)
        bit *= 2
    return out


def forward_kernel(S, F, nh, x_all, w, g1, sc, wz, n1, qt, kt, qn, kk, vn, ot, lse, mixed, wm,
                   wt, vt, xb, nb, wv, inx, outn, local, osend, orecv, wsend, wrecv):
    s, f, p, c = spots()
    P_ = S // 2
    T, D = x_all.shape[1], x_all.shape[2]
    C = nh * HD
    L = S * T
    BQ = 2 * T
    BK = min(512, BQ)
    other = 1 - c
    mate = (p * 2 + other, f)
    load = pltpu.make_async_copy(wz, wv, local.at[0])
    load.start()

    def fetch(b):
        return pltpu.make_async_copy(x_all.at[b], xb.at[lax.rem(b, 2)], inx.at[lax.rem(b, 2)])

    def store(b):
        return pltpu.make_async_copy(nb.at[lax.rem(b, 2)], n1.at[b], outn.at[lax.rem(b, 2)])

    fetch(0).start()
    greet(S, F)
    load.wait()
    keep = pltpu.make_async_copy(wv, wm.at[:, s], local.at[0])
    keep.start()

    zero = s - s
    chips = [flip_bits(p, i) for i in range(P_)]

    def num(n):
        return zero + n

    def spread(i):
        return remote(wv, wm.at[:, s], wsend, wrecv, i, (xor(p, i, P_) * 2 + c, f))

    def forward(i):
        src = xor(p, i, P_) * 2 + c
        n = (7 if P_ == 4 else P_) + i
        return remote(wm.at[:, src], wm.at[:, src], wsend, wrecv, n, mate)

    def part_of(src, half):
        return wm.at[:, src, pl.ds(num(half * (F // 2)), F // 2)]

    def direct(i, half):
        src = wv.at[:, pl.ds(half * (F // 2), F // 2)]
        to = (flip_bits(p, i) * 2 + c, f)
        return remote(src, part_of(s, half), wsend, wrecv, 2 * i + half, to)

    def arrived(i, half):
        blk = part_of(chips[i] * 2 + c, half)
        remote(blk, blk, wsend, wrecv, num(2 * i + half), mate).wait_recv()

    def relay(i):
        blk = part_of(flip_bits(p, i) * 2 + c, i - 1)
        return remote(blk, blk, wsend, wrecv, 5 + i, (flip_bits(p, 3 - i) * 2 + c, f))

    def relayed(half):
        blk = part_of(chips[3] * 2 + c, half)
        return remote(blk, blk, wsend, wrecv, num(6 + half), mate)

    def corner(half, core):
        blk = part_of(chips[3] * 2 + core, half)
        return remote(blk, blk, wsend, wrecv, num(10 + half), mate)

    square = P_ == 4
    if square:
        for first in range(2):
            for i in (1, 2):
                direct(i, first if i == 1 else 1 - first).start()
    else:
        for i in range(1, P_):
            spread(P_ - i).start()
    near = remote(wv, wm.at[:, s], wsend, wrecv, 0, mate)
    near.start()
    wt[...] = jnp.transpose(w[...])

    rows = 64

    def project(b, _):
        slot = lax.rem(b, 2)
        fetch(b).wait()

        @pl.when(b + 1 < S)
        def _():
            fetch(b + 1).start()

        @pl.when(b >= 2)
        def _():
            store(b - 2).wait()

        def norm(k, _):
            at = pl.ds(pl.multiple_of(k * rows, rows), rows)
            v = xb[slot, at, :].astype(f32)
            r = lax.rsqrt(jnp.mean(v * v, axis=-1, keepdims=True) + eps_norm)
            nb[slot, at, :] = (v * r * g1[...]).astype(bf)
            return 0

        lax.fori_loop(0, T // rows, norm, 0)
        store(b).start()
        cols = pl.ds(pl.multiple_of(b * T, T), T)
        res = dot(wt[...], nb[slot], 1, 1)
        qt[:, cols] = (res[:C] * sc[...]).astype(bf)
        kt[:, cols] = res[C : 2 * C].astype(bf)
        vt[:, cols] = res[2 * C :].astype(bf)
        for h in range(nh):
            part = slice(h * HD, (h + 1) * HD)
            qn[h, cols, :] = jnp.transpose(res[:C][part] * sc[part]).astype(bf)
            kk[h, cols, :] = jnp.transpose(res[C : 2 * C][part]).astype(bf)
            vn[h, cols, :] = jnp.transpose(res[2 * C :][part]).astype(bf)
        return 0

    lax.fori_loop(0, S, project, 0)
    if square:
        for i in (1, 2):
            arrived(i, i - 1)
            relay(i).start()
    store(S - 2).wait()
    store(S - 1).wait()

    r = BQ // BK

    def attend(t):
        first = pl.multiple_of(t * BQ, BQ)
        q = [qt[h * HD : (h + 1) * HD, pl.ds(first, BQ)] for h in range(nh)]

        def step(j, carry, diag=None):
            at = pl.ds(pl.multiple_of(j * BK, BK), BK)
            scores = [dot(kk[h, at, :], q[h]) for h in range(nh)]
            out = []
            for h in range(nh):
                m, l, acc = carry[h]
                sh = scores[h]
                if diag is not None:
                    kp = lax.broadcasted_iota(jnp.int32, sh.shape, 0) + diag * BK
                    qp = lax.broadcasted_iota(jnp.int32, sh.shape, 1)
                    sh = jnp.where(kp <= qp, sh, NEG)
                mn = jnp.maximum(m, jnp.max(sh, axis=0, keepdims=True))
                a = jnp.exp(m - mn)
                e = jnp.exp(sh - mn)
                l = l * a + jnp.sum(e, axis=0, keepdims=True)
                acc = acc * a + dot(vt[h * HD : (h + 1) * HD, at], e.astype(bf))
                out.append((mn, l, acc))
            return tuple(out)

        carry = tuple(
            (jnp.full((1, BQ), NEG, f32), jnp.zeros((1, BQ), f32), jnp.zeros((HD, BQ), f32))
            for _ in range(nh)
        )
        carry = lax.fori_loop(0, t * r, step, carry)
        for d in range(r):
            carry = step(t * r + d, carry, d)
        for h in range(nh):
            m, l, acc = carry[h]
            ot[h * HD : (h + 1) * HD, pl.ds(first, BQ)] = (acc / l).astype(bf)
            lse[h : h + 1, pl.ds(first, BQ)] = m + jnp.log(l)

    def to_owner(src, n, i, to):
        return pltpu.make_async_remote_copy(
            src_ref=src,
            dst_ref=mixed.at[s],
            send_sem=osend.at[n],
            recv_sem=orecv.at[2 * i + c],
            device_id=to,
            device_id_type=MESH,
        )

    def send(i, half):
        t = xor(p, i, P_)
        src = ot.at[:, pl.ds(pl.multiple_of(t * BQ + half * T, T), T)]
        return to_owner(src, 2 * i + half, i, (t * 2 + half, f))

    def turn(n, _):
        i = P_ - 1 - n
        attend(xor(p, i, P_))
        send(i, 0).start()
        send(i, 1).start()
        if not square:
            spread(i).wait_recv()
            forward(i).start()
            return 0

        @pl.when(i == 3)
        def _():
            arrived(2, 0)
            forward(num(2)).start()

        @pl.when(i == 2)
        def _():
            arrived(1, 1)
            forward(num(1)).start()

        @pl.when(i == 1)
        def _():
            for half in range(2):
                relayed(half).wait_recv()
                corner(half, c).start()

        return 0

    lax.fori_loop(0, P_ - 1, turn, 0)
    attend(p)
    mine = ot.at[:, pl.ds(pl.multiple_of(s * T, T), T)]
    theirs = ot.at[:, pl.ds(pl.multiple_of((p * 2 + other) * T, T), T)]
    last = to_owner(theirs, 0, 0, mate)
    last.start()
    own = pltpu.make_async_copy(mine, mixed.at[s], local.at[1])
    own.start()
    def from_source(i, core):
        return pltpu.make_async_remote_copy(
            src_ref=mine,
            dst_ref=mixed.at[flip_bits(p, i) * 2 + core],
            send_sem=osend.at[0],
            recv_sem=orecv.at[2 * i + core],
            device_id=mate,
            device_id_type=MESH,
        )

    for i in range(1, P_):
        for core in range(2):
            from_source(i, core).wait_recv()
    from_source(0, other).wait_recv()
    last.wait_send()
    own.wait()
    keep.wait()
    near.wait()
    if square:
        for i in (1, 2):
            forward(i).wait()
            relay(i).wait_send()
            for half in range(2):
                direct(i, half).wait_send()
        for half in range(2):
            corner(half, c).wait_send()
            corner(half, other).wait_recv()
    for i in range(1, P_):
        if not square:
            forward(i).wait()
            spread(i).wait_send()
        send(i, 0).wait_send()
        send(i, 1).wait_send()


def forward_all(S, F, nh, x_all, w, g1, sc, wz):
    T, D = x_all.shape[1], x_all.shape[2]
    C = nh * HD
    L = S * T
    P_ = S // 2
    any_ = pl.BlockSpec(memory_space=pl.ANY)
    vm = pl.BlockSpec(memory_space=pltpu.VMEM)
    dma = pltpu.SemaphoreType.DMA
    shape = jax.ShapeDtypeStruct
    NW, R = wz.shape[0], wz.shape[2]
    V = pltpu.VMEM
    return pl.pallas_call(
        functools.partial(forward_kernel, S, F, nh),
        out_shape=[
            shape((S, T, D), bf),
            shape((C, L), bf),
            shape((C, L), bf),
            shape((nh, L, HD), bf),
            shape((nh, L, HD), bf),
            shape((nh, L, HD), bf),
            shape((C, L), bf),
            shape((nh, L), f32),
            shape((S, C, T), bf),
            shape((NW, S, F, R, D), bf),
        ],
        in_specs=[any_, vm, vm, vm, any_],
        out_specs=[any_] + [vm] * 7 + [any_, any_],
        scratch_shapes=[
            V((3 * C, D), bf),
            V((C, L), bf),
            V((2, T, D), bf),
            V((2, T, D), bf),
            V((NW, F, R, D), bf),
            dma((2,)),
            dma((2,)),
            dma((2,)),
            dma((2 * P_,)),
            dma((2 * P_,)),
            dma((max(2 * P_, 12),)),
            dma((max(2 * P_, 12),)),
        ],
        compiler_params=pltpu.CompilerParams(
            collective_id=3, has_side_effects=True, vmem_limit_bytes=60 << 20
        ),
        name="forward",
    )(x_all, w, g1, sc, wz)


def middle_kernel(S, F, nh, mixed, x, ct, wm, small, out, dx2, dm, gi, vec,
                  mx, lt, xv, cv, wv, x2, n2, dn, ab, ub, eb, r2, sb, rb, ob, dov, rv, local, wsem,
                  dsend, drecv, gsend, grecv):
    s, f, p, c = spots()
    P_ = S // 2
    T, D = x.shape
    C = nh * HD
    NW = wm.shape[0]
    G = D // S
    other = 1 - c
    mate = (p * 2 + other, f)
    wide = 256 if D % 256 == 0 else D
    rows = 64
    loads = [
        pltpu.make_async_copy(mixed, mx, local.at[0]),
        pltpu.make_async_copy(x, xv, local.at[1]),
        pltpu.make_async_copy(ct, cv, local.at[2]),
    ]
    loads += [pltpu.make_async_copy(wm.at[n], wv.at[n], wsem.at[n]) for n in range(NW)]
    for load in loads:
        load.start()
    greet(S, F)
    g2, b1, b2 = small[1:2, :], small[2:3, :], small[3:4, :]

    def by_core(n, tall):
        for t in range(P_):
            for core in range(2):
                at = (t * 2 + core) * G
                lt[n, core, t * G : (t + 1) * G, :] = tall[at : at + G]

    def chunk(n):
        return pl.ds(pl.multiple_of(n * wide, wide), wide)

    def over(n, body):
        def one(k, _):
            body(k)
            return 0

        lax.fori_loop(0, n, one, 0)

    def lines(n):
        return pl.ds(pl.multiple_of(n * rows, rows), rows)

    loads[0].wait()
    tall = mx[...].reshape(D, T)
    by_core(0, tall)
    ub[...] = jnp.transpose(tall)
    loads[1].wait()
    loads[2].wait()
    loads[3].wait()

    def attend_out(n):
        at = chunk(n)
        x2[:, at] = xv[:, at].astype(f32) + dot(ub[...], wv[0, :, at])

    over(D // wide, attend_out)

    def norm(n):
        at = lines(n)
        z = x2[at, :]
        r = lax.rsqrt(jnp.mean(z * z, axis=-1, keepdims=True) + eps_norm)
        r2[at, :] = r
        n2[at, :] = (z * r * g2).astype(bf)

    over(T // rows, norm)
    loads[4].wait()
    loads[5].wait()
    rv[...] = jnp.zeros_like(rv)

    def hidden(n):
        at = chunk(n)
        u = dot(n2[...], wv[1, :, at]) + small[2:3, at]
        gate = 1 / (1 + jnp.exp(-u))
        ab[:, at] = (u * gate).astype(bf)
        ga = dot(cv[...], wv[2, at, :], 1, 1)
        du = ga * (gate * (1 + u * (1 - gate)))
        rv[2:3, at] = jnp.sum(du, axis=0, keepdims=True)
        ub[:, at] = du.astype(bf)
        rv[3:4, at] = jnp.sum(cv[:, at].astype(f32), axis=0, keepdims=True)

    over(D // wide, hidden)

    def up_back(n):
        at = chunk(n)
        dn[:, at] = dot(ub[...], wv[1, at, :], 1, 1)

    over(D // wide, up_back)

    def second(n):
        at = lines(n)
        z, r, d = x2[at, :], r2[at, :], dn[at, :]
        e = d * g2
        tilt = jnp.mean(e * z, axis=-1, keepdims=True)
        v = cv[at, :].astype(f32) + r * e - z * (r * r * r * tilt)
        rv[1:2, :] += jnp.sum(d * z * r, axis=0, keepdims=True)
        dn[at, :] = v
        eb[at, :] = v.astype(bf)

    over(T // rows, second)
    keep = pltpu.make_async_copy(dn, dx2, local.at[0])
    keep.start()

    def head_out(i, to):
        return remote(dov.at[i], dm.at[s], dsend, drecv, i, (to, f))

    def heads(i, _):
        to = lax.rem(s + i, S)
        rows_of = pl.ds(pl.multiple_of(to * C, C), C)
        dov[i] = dot(wv[0, rows_of, :], eb[...], 1, 1).astype(bf)

        head_out(i, to).start()
        return 0

    lax.fori_loop(1, S, heads, 0)
    mine = pl.ds(pl.multiple_of(s * C, C), C)
    dov[0] = dot(wv[0, mine, :], eb[...], 1, 1).astype(bf)
    home = pltpu.make_async_copy(dov.at[0], dm.at[s], local.at[1])
    home.start()

    by_core(1, jnp.transpose(n2[...]))
    by_core(2, jnp.transpose(ab[...]))
    right = [eb, ub, cv]

    def pass_on(n):
        return remote(sb.at[n], rb.at[n], gsend, grecv, n, mate)

    for n in range(NW):

        def send_side(k, n=n):
            at = chunk(k)
            sb[n, :, at] = dot(lt[n, other], right[n][:, at]).astype(bf)

        over(D // wide, send_side)
        pass_on(n).start()

    def top(n):
        at = chunk(n)
        y = x2[:, at] + dot(ab[...], wv[2, :, at]) + small[3:4, at]
        xv[:, at] = y.astype(bf)

    over(D // wide, top)
    done = pltpu.make_async_copy(xv, out, local.at[2])
    done.start()
    for n in range(NW):
        pass_on(n).wait_recv()

        def keep_side(k, n=n):
            at = chunk(k)
            both = dot(lt[n, c], right[n][:, at]) + rb[n, :, at].astype(f32)
            ob[n, :, at] = both.astype(bf)

        over(D // wide, keep_side)
    stores = []
    for i in range(P_):
        here = pl.ds(pl.multiple_of(flip_bits(p, i) * G, G), G)
        stores.append(pltpu.make_async_copy(ob.at[:, here], gi.at[i], wsem.at[i]))
        stores[-1].start()
    vec[...] = rv[...]
    for i in range(1, S):
        remote(dov.at[0], dm.at[lax.rem(s + S - i, S)], dsend, drecv, i, mate).wait_recv()
    for store in stores:
        store.wait()
    keep.wait()
    home.wait()
    done.wait()
    for i in range(1, S):
        head_out(i, lax.rem(s + i, S)).wait_send()
    for n in range(NW):
        pass_on(n).wait_send()


def middle_all(S, F, nh, mixed, x, ct, wm, small):
    T, D = x.shape
    C = nh * HD
    P_ = S // 2
    NW = wm.shape[0]
    G = D // S
    any_ = pl.BlockSpec(memory_space=pl.ANY)
    vm = pl.BlockSpec(memory_space=pltpu.VMEM)
    dma = pltpu.SemaphoreType.DMA
    shape = jax.ShapeDtypeStruct
    V = pltpu.VMEM
    return pl.pallas_call(
        functools.partial(middle_kernel, S, F, nh),
        out_shape=[
            shape((T, D), bf),
            shape((T, D), f32),
            shape((S, C, T), bf),
            shape((P_, NW, G, D), bf),
            shape((8, D), f32),
        ],
        in_specs=[any_, any_, any_, any_, vm],
        out_specs=[any_, any_, any_, any_, vm],
        scratch_shapes=[
            V((S, C, T), bf),
            V((NW, 2, P_ * G, T), bf),
            V((T, D), bf),
            V((T, D), bf),
            V((NW, D, D), bf),
            V((T, D), f32),
            V((T, D), bf),
            V((T, D), f32),
            V((T, D), bf),
            V((T, D), bf),
            V((T, D), bf),
            V((T, 1), f32),
            V((NW, P_ * G, D), bf),
            V((NW, P_ * G, D), bf),
            V((NW, P_ * G, D), bf),
            V((S, C, T), bf),
            V((8, D), f32),
            dma((3,)),
            dma((max(NW, P_),)),
            dma((S,)),
            dma((S,)),
            dma((NW,)),
            dma((NW,)),
        ],
        compiler_params=pltpu.CompilerParams(
            collective_id=5, has_side_effects=True, vmem_limit_bytes=64_000_000
        ),
        name="middle",
    )(mixed, x, ct, wm, small)


def backward_kernel(S, F, nh, dm, qt, kt, q, k, v, ot, lse, n1, x_all, w, sc, g1, gi, vec, dx2,
                    g_out, in_out, q_out, vec_out, gp, gr_, gj,
                    dmt, wt, dwt, fm, tm, nx, xx, rr, mb, own, bi, bp, rl, ga, gb, gz, qi, qo,
                    vi, vz, vp, gf, gs_, local, nsem, bload,
                    gsend, grecv, bsend, brecv, qsend, qrecv, vsend, vrecv):
    s, f, p, c = spots()
    P_ = S // 2
    T, D = x_all.shape[1], x_all.shape[2]
    C = nh * HD
    L = S * T
    BQ = 2 * T
    BK = min(512, BQ)
    NW, R = gi.shape[1], gi.shape[3]
    other = 1 - c
    mate = (p * 2 + other, f)
    todo = []

    def go(copy):
        copy.start()
        todo.append(copy)

    chips = [flip_bits(p, i) for i in range(P_)]
    zero = s - s

    def num(n):
        return zero + n

    def chip(i):
        return chips[i]

    deeps = [lax.rem(f + i, F) for i in range(F)]

    def deep(i):
        return deeps[i]

    def head(ref, h, at):
        return ref[h * HD : (h + 1) * HD, at]

    loads = [
        pltpu.make_async_copy(dm.at[b], dmt.at[:, b * T : (b + 1) * T], bload.at[b])
        for b in range(S)
    ]
    for load in loads:
        load.start()
    greet(S, F)

    order = list(range(P_ - 1, -1, -1))
    wt[...] = jnp.transpose(w[...])
    dwt[...] = jnp.zeros_like(dwt)
    gf[...] = jnp.zeros_like(gf)
    gs_[...] = jnp.zeros_like(gs_)
    for load in loads:
        load.wait()

    def slabs(body):
        def one(n, _):
            body(lax.div(n, F), lax.rem(n, F))
            return 0

        lax.fori_loop(0, NW * F, one, 0)

    square = P_ == 4
    ZG = 10 if square else 2 * P_
    FH, H_ = F // 2, T // 2

    def half_g(ref, half):
        return ref.at[:, pl.ds(num(half * FH), FH)]

    def direct_g(i, half):
        src, dst = half_g(gi.at[num(i)], half), half_g(gp.at[num(i)], half)
        if half == 2 - i:
            src = gj.at[num(half)]
        return remote(src, dst, gsend, grecv, num(2 + 2 * i + half), (chip(i) * 2 + c, f))

    def relay_g(i):
        src = half_g(gi.at[num(3)], i - 1)
        return remote(src, gr_.at[num(i - 1)], gsend, grecv, num(7 + i), (chip(i) * 2 + c, f))

    def join_g(i):
        half = 2 - i
        la = pltpu.make_async_copy(half_g(gi.at[num(i)], half), half_g(ga, 0), local.at[num(1)])
        la.start()
        relay_g(3 - i).wait_recv()
        lb = pltpu.make_async_copy(gr_.at[num(half)], half_g(gb, 0), local.at[num(2)])
        lb.start()
        la.wait()
        lb.wait()

        def add(z, _):
            for a in range(NW):
                w_ = num(a)
                ga[w_, z] = (ga[w_, z].astype(f32) + gb[w_, z].astype(f32)).astype(bf)
            return 0

        lax.fori_loop(0, FH, add, 0)
        st = pltpu.make_async_copy(half_g(ga, 0), gj.at[num(half)], local.at[num(1)])
        st.start()
        st.wait()
        direct_g(i, half).start()

    def out_g(i):
        return remote(gi.at[i], gp.at[i], gsend, grecv, P_ + i, (chip(i) * 2 + c, f))

    if square:
        relay_g(1).start()
        relay_g(2).start()
        direct_g(2, 1).start()
        direct_g(1, 0).start()
    else:
        for i in order[:-1]:
            out_g(i).start()

    rows = 64
    wide = 256 if D % 256 == 0 else D

    def over(i):
        return remote(mb, bi.at[i], bsend, brecv, i, mate)

    def direct_b(i, half):
        part = pl.ds(pl.multiple_of(num(half * H_), H_), H_)
        src, dst = bi.at[num(i), part], bp.at[num(i - 1), part]
        return remote(src, dst, bsend, brecv, num(2 + 2 * i + half), (chip(i) * 2 + c, f))

    def relay_b(i):
        part = pl.ds(pl.multiple_of(num((i - 1) * H_), H_), H_)
        src = bi.at[num(3), part]
        return remote(src, rl.at[num(i - 1)], bsend, brecv, num(7 + i), (chip(i) * 2 + c, f))

    def join_b(i):
        half = 2 - i
        direct_b(i, 1 - half).start()
        relay_b(3 - i).wait_recv()
        few = min(rows, H_)

        def add(n, _):
            here = pl.ds(pl.multiple_of(half * H_ + n * few, few), few)
            there = pl.ds(pl.multiple_of(n * few, few), few)
            both = bi[num(i), here, :].astype(f32) + rl[num(half), there, :].astype(f32)
            bi[num(i), here, :] = both.astype(bf)
            return 0

        lax.fori_loop(0, H_ // few, add, 0)
        direct_b(i, half).start()

    def out_b(i, t):
        return pltpu.make_async_remote_copy(
            src_ref=bi.at[i],
            dst_ref=bp.at[i - 1],
            send_sem=bsend.at[P_ + i],
            recv_sem=brecv.at[P_ + i],
            device_id=(t * 2 + c, f),
            device_id_type=MESH,
        )

    def deep_g(i):
        src = ga.at[:, deep(i)]
        return remote(src, gz.at[i], gsend, grecv, ZG + i, (s, deep(i)))

    def plane_sums():
        la = pltpu.make_async_copy(gi.at[0], ga, local.at[1])
        la.start()
        la.wait()
        for i in order[1:-1] if square else order[:-1]:
            if square:
                direct_g(i, 0).wait_recv()
                direct_g(i, 1).wait_recv()
            else:
                out_g(i).wait_recv()
            lb = pltpu.make_async_copy(gp.at[i], gb, local.at[2])
            lb.start()
            lb.wait()

            def more(a, z):
                ga[a, z] = (ga[a, z].astype(f32) + gb[a, z].astype(f32)).astype(bf)

            slabs(more)
        for i in range(1, F):
            deep_g(i).start()

    def attention(do, delta, dqt, dk, dv):
        dqt[...] = jnp.zeros_like(dqt)
        dk[...] = jnp.zeros_like(dk)
        dv[...] = jnp.zeros_like(dv)

        def turn(b, _):
            at = pl.ds(pl.multiple_of(b * T, T), T)
            for h in range(nh):
                do[h, at, :] = jnp.transpose(head(dmt, h, at))
                prod = head(dmt, h, at).astype(f32) * head(ot, h, at).astype(f32)
                delta[h : h + 1, at] = jnp.sum(prod, axis=0, keepdims=True)
            return 0

        lax.fori_loop(0, S, turn, 0)

        def tile(q0, k0, masked):
            qa = pl.ds(q0, BK)
            ka = pl.ds(k0, BK)
            scores = [dot(k[h, ka, :], head(qt, h, qa)) for h in range(nh)]
            dps = [dot(v[h, ka, :], head(dmt, h, qa)) for h in range(nh)]
            for h in range(nh):
                e = jnp.exp(scores[h] - lse[h : h + 1, qa])
                if masked:
                    kp = lax.broadcasted_iota(jnp.int32, e.shape, 0)
                    qp = lax.broadcasted_iota(jnp.int32, e.shape, 1)
                    e = jnp.where(kp <= qp, e, 0.0)
                ds = (e * (dps[h] - delta[h : h + 1, qa])).astype(bf)
                dv[h, ka, :] += dot(e.astype(bf), do[h, qa, :])
                dk[h, ka, :] += dot(ds, q[h, qa, :])
                dqt[h * HD : (h + 1) * HD, qa] += dot(head(kt, h, ka), ds)

        r = BQ // BK

        def rect(qb, kb):
            def one(n, _):
                q0 = pl.multiple_of(qb * BQ + lax.div(n, r) * BK, BK)
                k0 = pl.multiple_of(kb * BQ + lax.rem(n, r) * BK, BK)
                tile(q0, k0, False)
                return 0

            lax.fori_loop(0, r * r, one, 0)

        def triangle(t):
            def one(n, _):
                at = pl.multiple_of(t * BQ + n * BK, BK)
                tile(at, at, True)

                def below(j, _):
                    tile(at, pl.multiple_of(t * BQ + j * BK, BK), False)
                    return 0

                lax.fori_loop(0, n, below, 0)
                return 0

            lax.fori_loop(0, r, one, 0)

        def fetch(t, half):
            b = t * 2 + half
            return (
                pltpu.make_async_copy(n1.at[b], nx, nsem.at[0]),
                pltpu.make_async_copy(x_all.at[b], xx, nsem.at[1]),
            )

        def finish(t, half, dst):
            for copy in fetch(t, half):
                copy.start()
            at = pl.ds(pl.multiple_of((t * 2 + half) * T, T), T)
            dqs = dqt[:, at].astype(bf)
            dqf = dqs.astype(f32)
            gs_[...] += jnp.sum(dqf * qt[:, at].astype(f32), axis=1, keepdims=True)
            fm[:C, :] = (dqf * sc[...]).astype(bf)
            for h in range(nh):
                fm[C + h * HD : C + (h + 1) * HD, :] = jnp.transpose(dk[h, at, :]).astype(bf)
                fm[2 * C + h * HD : 2 * C + (h + 1) * HD, :] = jnp.transpose(dv[h, at, :]).astype(bf)
            tm[...] = jnp.transpose(fm[...])
            for copy in fetch(t, half):
                copy.wait()

            def inverse(n, _):
                a = pl.ds(pl.multiple_of(n * rows, rows), rows)
                z = xx[a, :].astype(f32)
                rr[a, :] = lax.rsqrt(jnp.mean(z * z, axis=-1, keepdims=True) + eps_norm)
                return 0

            lax.fori_loop(0, T // rows, inverse, 0)

            def column(n, _):
                a = pl.ds(pl.multiple_of(n * wide, wide), wide)
                back = dot(tm[...], wt[:, a])
                dst[:, a] = back.astype(bf)
                hat = xx[:, a].astype(f32) * rr[...]
                gf[:, a] += jnp.sum(back * hat, axis=0, keepdims=True)
                dwt[:, a] += dot(fm[...], nx[:, a])
                return 0

            lax.fori_loop(0, D // wide, column, 0)

        def combine(i):
            def one(n, _):
                a = pl.ds(pl.multiple_of(n * rows, rows), rows)
                bi[i, a, :] = (bi[i, a, :].astype(f32) + own[a, :].astype(f32)).astype(bf)
                return 0

            lax.fori_loop(0, T // rows, one, 0)

        def advance(i, t, last):
            def pair(m, _):
                u = xor(p, m, P_)
                rect(jnp.maximum(t, u), jnp.minimum(t, u))
                return 0

            lax.fori_loop(0, i, pair, 0)
            triangle(t)
            if not last:

                @pl.when(i < P_ - 1)
                def _():
                    over(i + 1).wait_send()

            else:
                over(1).wait_send()
            finish(t, other, mb)
            over(i).start()
            finish(t, c, own)
            over(i).wait_recv()
            combine(i)
            if last:
                return
            if not square:
                out_b(i, t).start()
                return

            @pl.when(i == 3)
            def _():
                relay_b(1).start()
                relay_b(2).start()
                join_g(2)
                join_g(1)

            @pl.when(i == 2)
            def _():
                join_b(2)

            @pl.when(i == 1)
            def _():
                join_b(1)

        def stage(n, _):
            i = P_ - 1 - n
            advance(i, xor(p, i, P_), False)
            return 0

        lax.fori_loop(0, P_ - 1, stage, 0)
        plane_sums()
        advance(0, p, True)


    V = pltpu.VMEM
    pl.run_scoped(
        attention,
        V((nh, L, HD), bf),
        V((nh, L), f32),
        V((C, L), f32),
        V((nh, L, HD), f32),
        V((nh, L, HD), f32),
    )

    def closing(dw, up, qm, qs_, go_, vo):
        up_load = pltpu.make_async_copy(dx2, up, local.at[0])
        up_load.start()
        x_load = pltpu.make_async_copy(x_all.at[s], xx, nsem.at[1])
        x_load.start()
        vi[...] = vec[...]
        vi[0:1, :] = gf[...]
        turned = jnp.transpose(jnp.broadcast_to(gs_[...], (C, 128)))
        vi[4:5, 0:C] = turned[0:1, :]
        for i in range(1, F):
            go(remote(vi, vz.at[i], vsend, vrecv, i, (s, deep(i))))
        dw[...] = jnp.transpose(dwt[...])

        bunch = 8 // math.gcd(R, 8)

        def piece(n, _):
            part = dw[pl.ds(pl.multiple_of(n * (bunch * R), 8), bunch * R), :]
            for j in range(bunch):
                to = n * bunch + j
                qm[lax.div(to, F), lax.rem(to, F)] = part[j * R : (j + 1) * R].astype(bf)
            return 0

        lax.fori_loop(0, S * F // bunch, piece, 0)
        for i in range(1, F):
            go(remote(qm.at[:, deep(i)], qi.at[i], qsend, qrecv, i, (s, deep(i))))
        total = vi[...]
        for i in range(1, F):
            remote(vi, vz.at[i], vsend, vrecv, i, mate).wait_recv()
            total = total + vz[i]
        vp[0] = total
        for i in range(1, S):
            go(remote(vp.at[0], vp.at[i], vsend, vrecv, F - 1 + i, (lax.rem(s + i, S), f)))
        for i in range(1, F):
            remote(qm.at[:, f], qi.at[i], qsend, qrecv, i, mate).wait_recv()

        def sum_q(n, _):
            part = qm[n, f].astype(f32)
            for i in range(1, F):
                part = part + qi[i, n].astype(f32)
            qs_[n] = part.astype(bf)
            return 0

        lax.fori_loop(0, S, sum_q, 0)
        keep = pltpu.make_async_copy(qs_.at[s], qo.at[s], local.at[1])
        keep.start()
        for i in range(1, S):
            to = lax.rem(s + i, S)
            go(remote(qs_.at[to], qo.at[s], qsend, qrecv, F - 1 + i, (to, f)))
        up_load.wait()
        x_load.wait()
        over(0).wait_send()
        used = (1, 2) if square else range(1, P_)
        for i in used:
            if square:
                direct_b(i, 0).wait_recv()
                direct_b(i, 1).wait_recv()
            else:
                out_b(i, chip(i)).wait_recv()

        def below(n, _):
            a = pl.ds(pl.multiple_of(n * rows, rows), rows)
            back = bi[0, a, :].astype(f32)
            for i in used:
                back = back + bp[i - 1, a, :].astype(f32)
            z = xx[a, :].astype(f32)
            r1 = lax.rsqrt(jnp.mean(z * z, axis=-1, keepdims=True) + eps_norm)
            e1 = back * g1[...]
            tilt = jnp.mean(e1 * z, axis=-1, keepdims=True)
            mb[a, :] = (up[a, :] + r1 * e1 - z * (r1 * r1 * r1 * tilt)).astype(bf)
            return 0

        lax.fori_loop(0, T // rows, below, 0)
        outs = [pltpu.make_async_copy(mb, in_out, local.at[0])]
        outs[0].start()
        for i in range(1, F):
            remote(ga.at[:, f], gz.at[i], gsend, grecv, ZG + i, mate).wait_recv()
        for a in range(NW):
            part = ga[a, f].astype(f32)
            for i in range(1, F):
                part = part + gz[i, a].astype(f32)
            go_[a] = part
        outs.append(pltpu.make_async_copy(go_, g_out, local.at[2]))
        outs[1].start()
        total = vp[0]
        for i in range(1, S):
            remote(vp.at[0], vp.at[i], vsend, vrecv, F - 1 + i, mate).wait_recv()
            total = total + vp[i]
        vo[...] = total
        outs.append(pltpu.make_async_copy(vo, vec_out, nsem.at[0]))
        outs[2].start()
        for i in range(1, S):
            src = lax.rem(s + S - i, S)
            remote(qs_.at[0], qo.at[src], qsend, qrecv, F - 1 + i, mate).wait_recv()
        keep.wait()
        outs.append(pltpu.make_async_copy(qo, q_out, local.at[1]))
        outs[3].start()
        for out in outs:
            out.wait()
        for copy in todo:
            copy.wait_send()
        for i in range(1, F):
            deep_g(i).wait_send()
        for i in used:
            if square:
                relay_g(i).wait_send()
                relay_b(i).wait_send()
                for half in range(2):
                    direct_g(i, half).wait_send()
                    direct_b(i, half).wait_send()
            else:
                out_g(i).wait_send()
                out_b(i, chip(i)).wait_send()

    pl.run_scoped(
        closing,
        V((D, 3 * C), f32),
        V((T, D), f32),
        V((S, F, R, 3 * C), bf),
        V((S, R, 3 * C), bf),
        V((NW, R, D), f32),
        V(vec.shape, f32),
    )


def backward_all(S, F, nh, dm, qt, kt, q, k, v, ot, lse, n1, x_all, w, sc, g1, gi, vec, dx2):
    T, D = x_all.shape[1], x_all.shape[2]
    C = nh * HD
    L = S * T
    P_ = S // 2
    NW, R = gi.shape[1], gi.shape[3]
    any_ = pl.BlockSpec(memory_space=pl.ANY)
    vm = pl.BlockSpec(memory_space=pltpu.VMEM)
    dma = pltpu.SemaphoreType.DMA
    shape = jax.ShapeDtypeStruct
    V = pltpu.VMEM
    return pl.pallas_call(
        functools.partial(backward_kernel, S, F, nh),
        out_shape=[
            shape((NW, R, D), f32),
            shape((T, D), bf),
            shape((S, R, 3 * C), bf),
            shape(vec.shape, f32),
            shape((P_, NW, F, R, D), bf),
            shape((2, NW, F // 2, R, D), bf),
            shape((2, NW, F // 2, R, D), bf),
        ],
        in_specs=[any_] + [vm] * 7 + [any_, any_, vm, vm, vm, any_, vm, any_],
        out_specs=[any_] * 7,
        scratch_shapes=[
            V((C, L), bf),
            V((3 * C, D), bf),
            V((3 * C, D), f32),
            V((3 * C, T), bf),
            V((T, 3 * C), bf),
            V((T, D), bf),
            V((T, D), bf),
            V((T, 1), f32),
            V((T, D), bf),
            V((T, D), bf),
            V((P_, T, D), bf),
            V((2 if P_ == 4 else P_ - 1, T, D), bf),
            V((2, T // 2, D), bf),
            V((NW, F, R, D), bf),
            V((NW, F, R, D), bf),
            V((F, NW, R, D), bf),
            V((F, S, R, 3 * C), bf),
            V((S, R, 3 * C), bf),
            V(vec.shape, f32),
            V((F,) + vec.shape, f32),
            V((S,) + vec.shape, f32),
            V((1, D), f32),
            V((C, 1), f32),
            dma((3,)),
            dma((2,)),
            dma((S,)),
            dma((10 + 2 * P_ + F,)),
            dma((10 + 2 * P_ + F,)),
            dma((max(2 * P_, 10),)),
            dma((max(2 * P_, 10),)),
            dma((S + F,)),
            dma((S + F,)),
            dma((S + F,)),
            dma((S + F,)),
        ],
        compiler_params=pltpu.CompilerParams(
            collective_id=4, has_side_effects=True, vmem_limit_bytes=66_000_000
        ),
        name="backward",
    )(dm, qt, kt, q, k, v, ot, lse, n1, x_all, w, sc, g1, gi, vec, dx2)


def body(
    inputs,
    w_query,
    w_key,
    w_value,
    w_proj,
    w_up,
    w_down,
    gain_first,
    gain_second,
    bias_up,
    bias_down,
    query_scale,
    cotangent,
):
    groups = lax.axis_size("seq")
    rows_of = lax.axis_size("fsdp")
    nh = H // groups
    cols = nh * HD
    both = ("seq", "fsdp")
    tokens, width = inputs.shape[1], inputs.shape[2]
    length = tokens * groups
    shard = w_query.shape[0]
    x_low = inputs.reshape(tokens, width)
    qkv_rows = jnp.stack([w_query, w_key, w_value], 1).astype(bf).reshape(shard, 3, groups, cols)
    qkv_rows = qkv_rows.transpose(2, 0, 1, 3).reshape(groups, shard, 3 * cols)
    small = jnp.stack([gain_first, gain_second, bias_up, bias_down], 0)
    small = jnp.pad(small.astype(bf), ((0, 12), (0, 128 - shard)))
    weights = jnp.stack([w_proj, w_up, w_down], 0).astype(bf)
    x_all, qkv_w, small, weights = gather_all(groups, rows_of, x_low, qkv_rows, small, weights)
    qkv_w = qkv_w.reshape(width, 3 * cols)
    small = small[:, :, :4, :shard].transpose(2, 0, 1, 3).reshape(4, width).astype(f32)
    scale_dims = jax.nn.softplus(query_scale) * log_two_inverse / math.sqrt(HD)
    scale_cols = jnp.tile(scale_dims, nh)
    normed, qt, kt, q, k, v, ot, lse, mixed, weights = forward_all(
        groups, rows_of, nh, x_all, qkv_w, small[:1], scale_cols[:, None], weights
    )
    result, grad_middle, dm, pairs, vectors = middle_all(
        groups,
        rows_of,
        nh,
        mixed,
        x_low,
        cotangent.reshape(tokens, width),
        weights.reshape(3, width, width),
        small,
    )
    owned, grad_inputs, grad_qkv, vectors, *unused = backward_all(
        groups,
        rows_of,
        nh,
        dm,
        qt,
        kt,
        q,
        k,
        v,
        ot,
        lse,
        normed,
        x_all,
        qkv_w,
        scale_cols[:, None],
        small[:1],
        pairs.reshape(groups // 2, 3, rows_of, shard, width),
        vectors,
        grad_middle,
    )
    grad_qkv = grad_qkv.reshape(groups, shard, 3, cols).transpose(2, 1, 0, 3)
    grad_qkv = grad_qkv.reshape(3, shard, width).astype(f32)
    at = (lax.axis_index("seq") * rows_of + lax.axis_index("fsdp")) * shard
    mine = lax.dynamic_slice_in_dim(vectors, at, shard, 1)
    scale_total = jnp.sum(vectors[4, :cols].reshape(nh, HD), axis=0) / scale_dims
    grad_scale = scale_total * jax.nn.sigmoid(query_scale) * log_two_inverse / math.sqrt(HD)
    return (
        result.reshape(inputs.shape),
        grad_inputs.reshape(inputs.shape),
        grad_qkv[0],
        grad_qkv[1],
        grad_qkv[2],
        owned[0],
        owned[1],
        owned[2],
        mine[0],
        mine[1],
        mine[2],
        mine[3],
        grad_scale,
    )


def solution(mesh):
    return jax.shard_map(
        body,
        mesh=mesh,
        in_specs=(
            P("fsdp", "seq", None),
            P(("seq", "fsdp"), None),
            P(("seq", "fsdp"), None),
            P(("seq", "fsdp"), None),
            P(("seq", "fsdp"), None),
            P(("seq", "fsdp"), None),
            P(("seq", "fsdp"), None),
            P(("seq", "fsdp")),
            P(("seq", "fsdp")),
            P(("seq", "fsdp")),
            P(("seq", "fsdp")),
            P(),
            P("fsdp", "seq", None),
        ),
        out_specs=(
            P("fsdp", "seq", None),
            P("fsdp", "seq", None),
            P(("seq", "fsdp"), None),
            P(("seq", "fsdp"), None),
            P(("seq", "fsdp"), None),
            P(("seq", "fsdp"), None),
            P(("seq", "fsdp"), None),
            P(("seq", "fsdp"), None),
            P(("seq", "fsdp")),
            P(("seq", "fsdp")),
            P(("seq", "fsdp")),
            P(("seq", "fsdp")),
            P(),
        ),
        check_vma=False,
    )
```

profile of v0, /device:TPU:0, one launch (start us, length us, event | category | flops | bytes accessed | tf_op | source)
XLA Modules:
  0.0 353.3 jit_solution(13430869686695211607)
XLA Ops:
  0.7 0.7 convert_bitcast_fusion.4
  1.4 0.7 convert_bitcast_fusion.6
  2.7 1.1 convert_bitcast_fusion
  3.7 0.9 convert_bitcast_fusion.2
  4.7 0.8 pad_maximum_fusion.wm
  7.0 1.3 maximum_bitcast_fusion
  8.3 1.1 reshape.76.wq
  9.3 59.7 %gather.1 = (bf16[8,512,1280]{2,1,0:T(8,128)(2,1)}, bf16[8,4,40,480]{3,2,1,0:T(8,128)(2,1)}, bf16[8,4,16,128]{3,2,1,0:T(8,128)(2,1)}, bf16[3,4,40,1280]{3,2,1,0:T(8,128)(2,1)}) custom-call(bf16[512,1280]{1,0:T(8,128)(2,1)} %bitcast.49, bf16[8,40,480]{2,1,0:T(8,128)(2,1)} %reshape.76.wq, bf16[16,128]{1,0:T(8,128)(2,1)} %fusion.8.sm, ...), custom_call_target="tpu_custom_call" | custom-call | tf_op jit(solution)/shard_map/gather/pallas_call | solution.py:195
  69.0 0.9 convert_bitcast_fusion.3
  70.6 0.8 broadcast_in_dim_tile.5.sc
  71.4 68.1 %forward.1 = (bf16[8,512,1280]{2,1,0:T(8,128)(2,1)}, bf16[160,4096]{1,0:T(8,128)(2,1)}, bf16[160,4096]{1,0:T(8,128)(2,1)}, bf16[2,4096,80]{2,1,0:T(8,128)(2,1)},...) custom-call(bf16[8,512,1280]{2,1,0:T(8,128)(2,1)} %get-tuple-element, ...), custom_call_target="tpu_custom_call" | custom-call | tf_op jit(solution)/shard_map/forward/pallas_call | solution.py:486
  139.6 0.7 convert_element_type.25.small
  140.3 41.4 %middle.1 = (bf16[512,1280]{1,0:T(8,128)(2,1)}, f32[512,1280]{1,0:T(8,128)}, bf16[8,160,512]{2,1,0:T(8,128)(2,1)}, bf16[4,3,160,1280]{3,2,1,0:T(8,128)(2,1)}, f32[8,1280]{1,0:T(8,128)}) custom-call(bf16[8,160,512]{2,1,0:T(8,128)(2,1)} %get-tuple-element.40.mixed, bf16[512,1280]{1,0:T(8,128)(2,1)} %bitcast.50, bf16[512,1280]{1,0:T(8,128)(2,1)} %bitcast.53, ...), custom_call_target="tpu_custom_call" | custom-call | tf_op jit(solution)/shard_map/middle/pallas_call | solution.py:705
  181.8 159.8 %backward.1 = (f32[3,40,1280]{2,1,0:T(8,128)}, bf16[512,1280]{1,0:T(8,128)(2,1)}, bf16[8,40,480]{2,1,0:T(8,128)(2,1)}, f32[8,1280]{1,0:T(8,128)}, bf16[4,3,4,40,...) custom-call(bf16[8,160,512]{2,1,0:T(8,128)(2,1)} %get-tuple-element.43.dm, ...), custom_call_target="tpu_custom_call" | custom-call | tf_op jit(solution)/shard_map/backward/pallas_call | solution.py:1229
  341.6 1.9 reshape.83
  344.3 0.8 squeeze.30
  345.2 0.8 squeeze.31
  346.2 0.8 squeeze.32
  347.0 0.8 slice_bitcast_fusion
  347.8 0.8 constant_dynamic-slice_fusion
  349.1 0.7 slice_reduce_fusion.1
  350.5 1.1 copy.50
  351.6 0.7 copy-done.1
  352.3 1.1 copy.51
  (36 shorter events, 5.0 us)
Async XLA Ops:
  0.6 4.8 %copy-start.3 = (f32[40,1280]{1,0:T(8,128)S(1)}, f32[40,1280]{1,0:T(8,128)}, u32[]{:S(2)}) copy-start(f32[40,1280]{1,0:T(8,128)} %param.14) | copy-start | bytes 614404
  1.4 4.6 %copy-start.4 = (f32[40,1280]{1,0:T(8,128)S(1)}, f32[40,1280]{1,0:T(8,128)}, u32[]{:S(2)}) copy-start(f32[40,1280]{1,0:T(8,128)} %param.15) | copy-start | bytes 614404
  4.7 1.8 copy-start.5
  8.3 62.3 %copy-start.6 = (f32[80]{0:T(128)S(1)}, f32[80]{0:T(128)}, u32[]{:S(2)}) copy-start(f32[80]{0:T(128)} %param.24) | copy-start | bytes 964
  345.1 1.9 copy-start.2
  346.1 4.4 %copy-start = (bf16[512,1280]{1,0:T(8,128)(2,1)S(1)}, bf16[512,1280]{1,0:T(8,128)(2,1)}, u32[]{:S(2)}) copy-start(bf16[512,1280]{1,0:T(8,128)(2,1)} %get-tuple-element.42) | copy-start | bytes 3932164
  350.5 1.8 copy-start.1
where the time goes:
time: 359 us; the launch traced here: 353 us
  Pallas kernels  329 us (92%)
  local copies, waits for them, and re-layouts  15.9 us (4%)
  other arithmetic  7.52 us (2%)
    pallas_call x1, Pallas kernels, backward_all(): pl.pallas_call(functools.partial(backward_kernel, S, F, nh), out_shape=[s...  160 us
    pallas_call x1, Pallas kernels, forward_all(): pl.pallas_call(functools.partial(forward_kernel, S, F, nh), out_shape=[sh...  68.1 us
    pallas_call x1, Pallas kernels, gather_all(): pl.pallas_call(functools.partial(gather_kernel, S, F), out_shape=[jax.Sha...  59.7 us
    pallas_call x1, Pallas kernels, middle_all(): pl.pallas_call(functools.partial(middle_kernel, S, F, nh), out_shape=[sha...  41.4 us

commit v1 on v0

--- a/solution.py
+++ b/solution.py
@@ -521,8 +521,8 @@
 
 
 def middle_kernel(S, F, nh, mixed, x, ct, wm, small, out, dx2, dm, gi, vec,
-                  mx, lt, xv, cv, wv, x2, n2, dn, ab, ub, eb, r2, sb, rb, ob, dov, rv, local, wsem,
-                  dsend, drecv, gsend, grecv):
+                  mx, lt, xv, cv, wv, x2, n2, dn, ab, ub, eb, r2, sb, rb, ob, dov, rv, vz, vp, local, wsem,
+                  dsend, drecv, gsend, grecv, vsend, vrecv):
     s, f, p, c = spots()
     P_ = S // 2
     T, D = x.shape
@@ -622,6 +622,15 @@
     keep = pltpu.make_async_copy(dn, dx2, local.at[0])
     keep.start()
 
+    def vec_z(i):
+        return remote(rv, vz.at[i], vsend, vrecv, i, (s, lax.rem(f + i, F)))
+
+    def vec_s(i):
+        return remote(vp.at[0], vp.at[i], vsend, vrecv, F - 1 + i, (lax.rem(s + i, S), f))
+
+    for i in range(1, F):
+        vec_z(i).start()
+
     def head_out(i, to):
         return remote(dov.at[i], dm.at[s], dsend, drecv, i, (to, f))
 
@@ -654,6 +663,14 @@
 
         over(D // wide, send_side)
         pass_on(n).start()
+
+    part = rv[...]
+    for i in range(1, F):
+        vec_z(i).wait_recv()
+        part = part + vz[i]
+    vp[0] = part
+    for i in range(1, S):
+        vec_s(i).start()
 
     def top(n):
         at = chunk(n)
@@ -677,7 +694,15 @@
         here = pl.ds(pl.multiple_of(flip_bits(p, i) * G, G), G)
         stores.append(pltpu.make_async_copy(ob.at[:, here], gi.at[i], wsem.at[i]))
         stores[-1].start()
-    vec[...] = rv[...]
+    part = vp[0]
+    for i in range(1, S):
+        vec_s(i).wait_recv()
+        part = part + vp[i]
+    vec[...] = part
+    for i in range(1, F):
+        vec_z(i).wait_send()
+    for i in range(1, S):
+        vec_s(i).wait_send()
     for i in range(1, S):
         remote(dov.at[0], dm.at[lax.rem(s + S - i, S)], dsend, drecv, i, mate).wait_recv()
     for store in stores:
@@ -731,12 +756,16 @@
             V((NW, P_ * G, D), bf),
             V((S, C, T), bf),
             V((8, D), f32),
+            V((F, 8, D), f32),
+            V((S, 8, D), f32),
             dma((3,)),
             dma((max(NW, P_),)),
             dma((S,)),
             dma((S,)),
             dma((NW,)),
             dma((NW,)),
+            dma((S + F,)),
+            dma((S + F,)),
         ],
         compiler_params=pltpu.CompilerParams(
             collective_id=5, has_side_effects=True, vmem_limit_bytes=64_000_000
@@ -745,8 +774,8 @@
     )(mixed, x, ct, wm, small)
 
 
-def backward_kernel(S, F, nh, dm, qt, kt, q, k, v, ot, lse, n1, x_all, w, sc, g1, gi, vec, dx2,
-                    g_out, in_out, q_out, vec_out, gp, gr_, gj,
+def backward_kernel(S, F, nh, dm, qt, kt, q, k, v, ot, lse, n1, x_all, w, sc, g1, gi, dx2,
+                    o_proj, o_up, o_down, in_out, o_q, o_k, o_v, vec_out, gp, gr_, gj,
                     dmt, wt, dwt, fm, tm, nx, xx, rr, mb, own, bi, bp, rl, ga, gb, gz, qi, qo,
                     vi, vz, vp, gf, gs_, local, nsem, bload,
                     gsend, grecv, bsend, brecv, qsend, qrecv, vsend, vrecv):
@@ -846,7 +875,7 @@
         direct_g(i, half).start()
 
     def out_g(i):
-        return remote(gi.at[i], gp.at[i], gsend, grecv, P_ + i, (chip(i) * 2 + c, f))
+        return remote(gi.at[num(i)], gp.at[num(i)], gsend, grecv, num(P_ + i), (chip(i) * 2 + c, f))
 
     if square:
         relay_g(1).start()
@@ -862,6 +891,38 @@
 
     def over(i):
         return remote(mb, bi.at[i], bsend, brecv, i, mate)
+
+    def inverse(slot):
+        def one(n, _):
+            a = pl.ds(pl.multiple_of(n * rows, rows), rows)
+            z = xx[slot, a, :].astype(f32)
+            rr[a, :] = lax.rsqrt(jnp.mean(z * z, axis=-1, keepdims=True) + eps_norm)
+            return 0
+
+        lax.fori_loop(0, T // rows, one, 0)
+
+    def back_part(slot, a, dst):
+        back = dot(tm[slot], wt[:, a])
+        dst[:, a] = back.astype(bf)
+        hat = xx[slot, :, a].astype(f32) * rr[...]
+        gf[:, a] += jnp.sum(back * hat, axis=0, keepdims=True)
+
+    def finish_back(slot, dst):
+        inverse(slot)
+
+        def column(n, _):
+            back_part(slot, pl.ds(pl.multiple_of(n * wide, wide), wide), dst)
+            return 0
+
+        lax.fori_loop(0, D // wide, column, 0)
+
+    def combine(i):
+        def one(n, _):
+            a = pl.ds(pl.multiple_of(n * rows, rows), rows)
+            bi[i, a, :] = (bi[i, a, :].astype(f32) + own[a, :].astype(f32)).astype(bf)
+            return 0
+
+        lax.fori_loop(0, T // rows, one, 0)
 
     def direct_b(i, half):
         part = pl.ds(pl.multiple_of(num(half * H_), H_), H_)
@@ -901,10 +962,10 @@
 
     def deep_g(i):
         src = ga.at[:, deep(i)]
-        return remote(src, gz.at[i], gsend, grecv, ZG + i, (s, deep(i)))
+        return remote(src, gz.at[num(i)], gsend, grecv, num(ZG + i), (s, deep(i)))
 
     def plane_sums():
-        la = pltpu.make_async_copy(gi.at[0], ga, local.at[1])
+        la = pltpu.make_async_copy(gi.at[num(0)], ga, local.at[num(1)])
         la.start()
         la.wait()
         for i in order[1:-1] if square else order[:-1]:
@@ -913,14 +974,17 @@
                 direct_g(i, 1).wait_recv()
             else:
                 out_g(i).wait_recv()
-            lb = pltpu.make_async_copy(gp.at[i], gb, local.at[2])
+            lb = pltpu.make_async_copy(gp.at[num(i)], gb, local.at[num(2)])
             lb.start()
             lb.wait()
 
-            def more(a, z):
-                ga[a, z] = (ga[a, z].astype(f32) + gb[a, z].astype(f32)).astype(bf)
-
-            slabs(more)
+            def more(z, _):
+                for a in range(NW):
+                    w_ = num(a)
+                    ga[w_, z] = (ga[w_, z].astype(f32) + gb[w_, z].astype(f32)).astype(bf)
+                return 0
+
+            lax.fori_loop(0, F, more, 0)
         for i in range(1, F):
             deep_g(i).start()
 
@@ -980,16 +1044,20 @@
 
             lax.fori_loop(0, r, one, 0)
 
-        def fetch(t, half):
-            b = t * 2 + half
+        def fetch(t, slot):
+            b = t * 2 + ((other, c)[slot])
             return (
-                pltpu.make_async_copy(n1.at[b], nx, nsem.at[0]),
-                pltpu.make_async_copy(x_all.at[b], xx, nsem.at[1]),
+                pltpu.make_async_copy(n1.at[b], nx.at[slot], nsem.at[2 * slot]),
+                pltpu.make_async_copy(x_all.at[b], xx.at[slot], nsem.at[2 * slot + 1]),
             )
 
-        def finish(t, half, dst):
-            for copy in fetch(t, half):
-                copy.start()
+        def fetch_both(t):
+            for slot in range(2):
+                for copy in fetch(t, slot):
+                    copy.start()
+
+        def prepare(t, slot):
+            half = (other, c)[slot]
             at = pl.ds(pl.multiple_of((t * 2 + half) * T, T), T)
             dqs = dqt[:, at].astype(bf)
             dqf = dqs.astype(f32)
@@ -998,38 +1066,37 @@
             for h in range(nh):
                 fm[C + h * HD : C + (h + 1) * HD, :] = jnp.transpose(dk[h, at, :]).astype(bf)
                 fm[2 * C + h * HD : 2 * C + (h + 1) * HD, :] = jnp.transpose(dv[h, at, :]).astype(bf)
-            tm[...] = jnp.transpose(fm[...])
-            for copy in fetch(t, half):
+            tm[slot] = jnp.transpose(fm[...])
+            for copy in fetch(t, slot):
                 copy.wait()
 
-            def inverse(n, _):
-                a = pl.ds(pl.multiple_of(n * rows, rows), rows)
-                z = xx[a, :].astype(f32)
-                rr[a, :] = lax.rsqrt(jnp.mean(z * z, axis=-1, keepdims=True) + eps_norm)
-                return 0
-
-            lax.fori_loop(0, T // rows, inverse, 0)
+        def weight_part(slot, a):
+            dwt[:, a] += dot(fm[...], nx[slot, :, a])
+
+        def finish(t, slot, dst):
+            prepare(t, slot)
+            inverse(slot)
 
             def column(n, _):
                 a = pl.ds(pl.multiple_of(n * wide, wide), wide)
-                back = dot(tm[...], wt[:, a])
-                dst[:, a] = back.astype(bf)
-                hat = xx[:, a].astype(f32) * rr[...]
-                gf[:, a] += jnp.sum(back * hat, axis=0, keepdims=True)
-                dwt[:, a] += dot(fm[...], nx[:, a])
+                back_part(slot, a, dst)
+                weight_part(slot, a)
                 return 0
 
             lax.fori_loop(0, D // wide, column, 0)
 
-        def combine(i):
-            def one(n, _):
-                a = pl.ds(pl.multiple_of(n * rows, rows), rows)
-                bi[i, a, :] = (bi[i, a, :].astype(f32) + own[a, :].astype(f32)).astype(bf)
+        def finish_weights(t, slot):
+            prepare(t, slot)
+
+            def column(n, _):
+                weight_part(slot, pl.ds(pl.multiple_of(n * wide, wide), wide))
                 return 0
 
-            lax.fori_loop(0, T // rows, one, 0)
-
-        def advance(i, t, last):
+            lax.fori_loop(0, D // wide, column, 0)
+
+        def flash(i, t):
+            fetch_both(t)
+
             def pair(m, _):
                 u = xor(p, m, P_)
                 rect(jnp.maximum(t, u), jnp.minimum(t, u))
@@ -1037,21 +1104,29 @@
 
             lax.fori_loop(0, i, pair, 0)
             triangle(t)
-            if not last:
-
-                @pl.when(i < P_ - 1)
+
+        def advance(i, t):
+            @pl.when(i == 1)
+            def _():
+                plane_sums()
+
+            flash(i, t)
+            if square:
+
+                @pl.when(i == 3)
                 def _():
-                    over(i + 1).wait_send()
-
-            else:
-                over(1).wait_send()
-            finish(t, other, mb)
+                    join_g(2)
+                    join_g(1)
+
+            @pl.when(i < P_ - 1)
+            def _():
+                over(i + 1).wait_send()
+
+            finish(t, 0, mb)
             over(i).start()
-            finish(t, c, own)
+            finish(t, 1, own)
             over(i).wait_recv()
             combine(i)
-            if last:
-                return
             if not square:
                 out_b(i, t).start()
                 return
@@ -1060,8 +1135,6 @@
             def _():
                 relay_b(1).start()
                 relay_b(2).start()
-                join_g(2)
-                join_g(1)
 
             @pl.when(i == 2)
             def _():
@@ -1073,12 +1146,13 @@
 
         def stage(n, _):
             i = P_ - 1 - n
-            advance(i, xor(p, i, P_), False)
+            advance(i, xor(p, i, P_))
             return 0
 
         lax.fori_loop(0, P_ - 1, stage, 0)
-        plane_sums()
-        advance(0, p, True)
+        flash(0, p)
+        finish_weights(p, 0)
+        finish_weights(p, 1)
 
 
     V = pltpu.VMEM
@@ -1092,16 +1166,6 @@
     )
 
     def closing(dw, up, qm, qs_, go_, vo):
-        up_load = pltpu.make_async_copy(dx2, up, local.at[0])
-        up_load.start()
-        x_load = pltpu.make_async_copy(x_all.at[s], xx, nsem.at[1])
-        x_load.start()
-        vi[...] = vec[...]
-        vi[0:1, :] = gf[...]
-        turned = jnp.transpose(jnp.broadcast_to(gs_[...], (C, 128)))
-        vi[4:5, 0:C] = turned[0:1, :]
-        for i in range(1, F):
-            go(remote(vi, vz.at[i], vsend, vrecv, i, (s, deep(i))))
         dw[...] = jnp.transpose(dwt[...])
 
         bunch = 8 // math.gcd(R, 8)
@@ -1116,6 +1180,22 @@
         lax.fori_loop(0, S * F // bunch, piece, 0)
         for i in range(1, F):
             go(remote(qm.at[:, deep(i)], qi.at[i], qsend, qrecv, i, (s, deep(i))))
+        up_load = pltpu.make_async_copy(dx2, up, local.at[0])
+        up_load.start()
+        over(1).wait_send()
+        finish_back(0, mb)
+        over(0).start()
+        finish_back(1, own)
+        vi[0:1, :] = gf[...]
+        vi[1:2, :] = jnp.zeros_like(gf)
+        turned = jnp.transpose(jnp.broadcast_to(gs_[...], (C, 128)))
+        vi[1:2, 0:C] = turned[0:1, :]
+        for i in range(1, F):
+            go(remote(vi, vz.at[i], vsend, vrecv, i, (s, deep(i))))
+        x_load = pltpu.make_async_copy(x_all.at[s], xx.at[0], nsem.at[1])
+        x_load.start()
+        over(0).wait_recv()
+        combine(0)
         total = vi[...]
         for i in range(1, F):
             remote(vi, vz.at[i], vsend, vrecv, i, mate).wait_recv()
@@ -1155,7 +1235,7 @@
             back = bi[0, a, :].astype(f32)
             for i in used:
                 back = back + bp[i - 1, a, :].astype(f32)
-            z = xx[a, :].astype(f32)
+            z = xx[0, a, :].astype(f32)
             r1 = lax.rsqrt(jnp.mean(z * z, axis=-1, keepdims=True) + eps_norm)
             e1 = back * g1[...]
             tilt = jnp.mean(e1 * z, axis=-1, keepdims=True)
@@ -1172,21 +1252,26 @@
             for i in range(1, F):
                 part = part + gz[i, a].astype(f32)
             go_[a] = part
-        outs.append(pltpu.make_async_copy(go_, g_out, local.at[2]))
-        outs[1].start()
+        for a, ref in enumerate((o_proj, o_up, o_down)):
+            outs.append(pltpu.make_async_copy(go_.at[a], ref, bload.at[a]))
+            outs[-1].start()
         total = vp[0]
         for i in range(1, S):
             remote(vp.at[0], vp.at[i], vsend, vrecv, F - 1 + i, mate).wait_recv()
             total = total + vp[i]
         vo[...] = total
         outs.append(pltpu.make_async_copy(vo, vec_out, nsem.at[0]))
-        outs[2].start()
+        outs[-1].start()
         for i in range(1, S):
             src = lax.rem(s + S - i, S)
             remote(qs_.at[0], qo.at[src], qsend, qrecv, F - 1 + i, mate).wait_recv()
         keep.wait()
-        outs.append(pltpu.make_async_copy(qo, q_out, local.at[1]))
-        outs[3].start()
+        for a, ref in enumerate((o_q, o_k, o_v)):
+            for src in range(S):
+                part = qo[src, :, a * C : (a + 1) * C].astype(f32)
+                go_[NW + a, :, src * C : (src + 1) * C] = part
+            outs.append(pltpu.make_async_copy(go_.at[NW + a], ref, bload.at[NW + a]))
+            outs[-1].start()
         for out in outs:
             out.wait()
         for copy in todo:
@@ -1210,12 +1295,12 @@
         V((T, D), f32),
         V((S, F, R, 3 * C), bf),
         V((S, R, 3 * C), bf),
-        V((NW, R, D), f32),
-        V(vec.shape, f32),
+        V((NW + 3, R, D), f32),
+        V((2, D), f32),
     )
 
 
-def backward_all(S, F, nh, dm, qt, kt, q, k, v, ot, lse, n1, x_all, w, sc, g1, gi, vec, dx2):
+def backward_all(S, F, nh, dm, qt, kt, q, k, v, ot, lse, n1, x_all, w, sc, g1, gi, dx2):
     T, D = x_all.shape[1], x_all.shape[2]
     C = nh * HD
     L = S * T
@@ -1229,24 +1314,28 @@
     return pl.pallas_call(
         functools.partial(backward_kernel, S, F, nh),
         out_shape=[
-            shape((NW, R, D), f32),
+            shape((R, D), f32),
+            shape((R, D), f32),
+            shape((R, D), f32),
             shape((T, D), bf),
-            shape((S, R, 3 * C), bf),
-            shape(vec.shape, f32),
+            shape((R, D), f32),
+            shape((R, D), f32),
+            shape((R, D), f32),
+            shape((2, D), f32),
             shape((P_, NW, F, R, D), bf),
             shape((2, NW, F // 2, R, D), bf),
             shape((2, NW, F // 2, R, D), bf),
         ],
-        in_specs=[any_] + [vm] * 7 + [any_, any_, vm, vm, vm, any_, vm, any_],
-        out_specs=[any_] * 7,
+        in_specs=[any_] + [vm] * 7 + [any_, any_, vm, vm, vm, any_, any_],
+        out_specs=[any_] * 11,
         scratch_shapes=[
             V((C, L), bf),
             V((3 * C, D), bf),
             V((3 * C, D), f32),
             V((3 * C, T), bf),
-            V((T, 3 * C), bf),
-            V((T, D), bf),
-            V((T, D), bf),
+            V((2, T, 3 * C), bf),
+            V((2, T, D), bf),
+            V((2, T, D), bf),
             V((T, 1), f32),
             V((T, D), bf),
             V((T, D), bf),
@@ -1258,13 +1347,13 @@
             V((F, NW, R, D), bf),
             V((F, S, R, 3 * C), bf),
             V((S, R, 3 * C), bf),
-            V(vec.shape, f32),
-            V((F,) + vec.shape, f32),
-            V((S,) + vec.shape, f32),
+            V((2, D), f32),
+            V((F, 2, D), f32),
+            V((S, 2, D), f32),
             V((1, D), f32),
             V((C, 1), f32),
             dma((3,)),
-            dma((2,)),
+            dma((4,)),
             dma((S,)),
             dma((10 + 2 * P_ + F,)),
             dma((10 + 2 * P_ + F,)),
@@ -1279,7 +1368,7 @@
             collective_id=4, has_side_effects=True, vmem_limit_bytes=66_000_000
         ),
         name="backward",
-    )(dm, qt, kt, q, k, v, ot, lse, n1, x_all, w, sc, g1, gi, vec, dx2)
+    )(dm, qt, kt, q, k, v, ot, lse, n1, x_all, w, sc, g1, gi, dx2)
 
 
 def body(
@@ -1329,7 +1418,17 @@
         weights.reshape(3, width, width),
         small,
     )
-    owned, grad_inputs, grad_qkv, vectors, *unused = backward_all(
+    (
+        grad_proj,
+        grad_up,
+        grad_down,
+        grad_inputs,
+        grad_query,
+        grad_key,
+        grad_value,
+        late,
+        *unused,
+    ) = backward_all(
         groups,
         rows_of,
         nh,
@@ -1347,24 +1446,22 @@
         scale_cols[:, None],
         small[:1],
         pairs.reshape(groups // 2, 3, rows_of, shard, width),
-        vectors,
         grad_middle,
     )
-    grad_qkv = grad_qkv.reshape(groups, shard, 3, cols).transpose(2, 1, 0, 3)
-    grad_qkv = grad_qkv.reshape(3, shard, width).astype(f32)
     at = (lax.axis_index("seq") * rows_of + lax.axis_index("fsdp")) * shard
+    vectors = jnp.concatenate([late[:1], vectors[1:4]], 0)
     mine = lax.dynamic_slice_in_dim(vectors, at, shard, 1)
-    scale_total = jnp.sum(vectors[4, :cols].reshape(nh, HD), axis=0) / scale_dims
+    scale_total = jnp.sum(late[1, :cols].reshape(nh, HD), axis=0) / scale_dims
     grad_scale = scale_total * jax.nn.sigmoid(query_scale) * log_two_inverse / math.sqrt(HD)
     return (
         result.reshape(inputs.shape),
         grad_inputs.reshape(inputs.shape),
-        grad_qkv[0],
-        grad_qkv[1],
-        grad_qkv[2],
-        owned[0],
-        owned[1],
-        owned[2],
+        grad_query,
+        grad_key,
+        grad_value,
+        grad_proj,
+        grad_up,
+        grad_down,
         mine[0],
         mine[1],
         mine[2],

time: 359 us -> 334 us (0.930); the launches traced: 353 us -> 334 us
  Pallas kernels: 329 us -> 311 us
    pallas_call x1, Pallas kernels: 160 us -> 139 us  [backward_all(): pl.pallas_call(functools.partial(backward_kernel, S, F, nh), out_shape=[s...]
    unnamed x16 -> x32, local copies, waits for them, and re-layouts: 2.87 us -> 7.75 us
where the time goes in v1:
time: 334 us
  Pallas kernels  311 us (93%)
  local copies, waits for them, and re-layouts  14.5 us (4%)
  other arithmetic  7.6 us (2%)
    pallas_call x1, Pallas kernels, backward_all(): pl.pallas_call(functools.partial(backward_kernel, S, F, nh), out_shape=[s...  139 us
    pallas_call x1, Pallas kernels, forward_all(): pl.pallas_call(functools.partial(forward_kernel, S, F, nh), out_shape=[sh...  68.1 us
    pallas_call x1, Pallas kernels, gather_all(): pl.pallas_call(functools.partial(gather_kernel, S, F), out_shape=[jax.Sha...  59.7 us
    pallas_call x1, Pallas kernels, middle_all(): pl.pallas_call(functools.partial(middle_kernel, S, F, nh), out_shape=[sha...  43.7 us
    unnamed x32, local copies, waits for them, and re-layouts  7.75 us

profile of v1, /device:TPU:0, one launch (start us, length us, event | category | flops | bytes accessed | tf_op | source)
XLA Modules:
  0.0 333.7 jit_solution(10577920534955476049)
XLA Ops:
  0.7 0.7 convert_bitcast_fusion.4
  1.4 0.7 convert_bitcast_fusion.6
  2.7 1.1 convert_bitcast_fusion
  3.7 0.9 convert_bitcast_fusion.2
  4.7 0.8 pad_maximum_fusion.wm
  7.0 1.3 maximum_bitcast_fusion
  8.3 1.1 reshape.65.wq
  9.3 59.7 %gather.1 = (bf16[8,512,1280]{2,1,0:T(8,128)(2,1)}, bf16[8,4,40,480]{3,2,1,0:T(8,128)(2,1)}, bf16[8,4,16,128]{3,2,1,0:T(8,128)(2,1)}, bf16[3,4,40,1280]{3,2,1,0:T(8,128)(2,1)}) custom-call(bf16[512,1280]{1,0:T(8,128)(2,1)} %bitcast.36, bf16[8,40,480]{2,1,0:T(8,128)(2,1)} %reshape.65.wq, bf16[16,128]{1,0:T(8,128)(2,1)} %fusion.8.sm, ...), custom_call_target="tpu_custom_call" | custom-call | tf_op jit(solution)/shard_map/gather/pallas_call | solution.py:195
  69.0 0.9 convert_bitcast_fusion.3
  69.9 0.7 slice.33.g1
  70.6 0.8 broadcast_in_dim_tile.5.sc
  71.4 68.1 %forward.1 = (bf16[8,512,1280]{2,1,0:T(8,128)(2,1)}, bf16[160,4096]{1,0:T(8,128)(2,1)}, bf16[160,4096]{1,0:T(8,128)(2,1)}, bf16[2,4096,80]{2,1,0:T(8,128)(2,1)},...) custom-call(bf16[8,512,1280]{2,1,0:T(8,128)(2,1)} %get-tuple-element, ...), custom_call_target="tpu_custom_call" | custom-call | tf_op jit(solution)/shard_map/forward/pallas_call | solution.py:486
  139.6 0.7 convert_element_type.15.small
  140.3 43.7 %middle.1 = (bf16[512,1280]{1,0:T(8,128)(2,1)}, f32[512,1280]{1,0:T(8,128)}, bf16[8,160,512]{2,1,0:T(8,128)(2,1)}, bf16[4,3,160,1280]{3,2,1,0:T(8,128)(2,1)}, f32[8,1280]{1,0:T(8,128)}) custom-call(bf16[8,160,512]{2,1,0:T(8,128)(2,1)} %get-tuple-element.44.mixed, bf16[512,1280]{1,0:T(8,128)(2,1)} %bitcast.37, bf16[512,1280]{1,0:T(8,128)(2,1)} %bitcast.39, ...), custom_call_target="tpu_custom_call" | custom-call | tf_op jit(solution)/shard_map/middle/pallas_call | solution.py:730
  184.0 139.2 %backward.1 = (f32[40,1280]{1,0:T(8,128)}, f32[40,1280]{1,0:T(8,128)}, f32[40,1280]{1,0:T(8,128)}, bf16[512,1280]{1,0:T(8,128)(2,1)}, f32[40,1280]{1,0:T(8,128)}...) custom-call(bf16[8,160,512]{2,1,0:T(8,128)(2,1)} %get-tuple-element., ...), custom_call_target="tpu_custom_call" | custom-call | tf_op jit(solution)/shard_map/backward/pallas_call | solution.py:1314
  323.3 0.7 slice.34
  325.9 2.6 copy.44
  328.5 1.1 copy.45
  329.6 0.7 copy.46
  330.3 0.7 copy.47
  331.0 0.7 copy.48
  331.6 0.7 copy.49
  332.3 0.7 copy.50
  333.0 0.7 copy.51
  (45 shorter events, 4.1 us)
Async XLA Ops:
  0.6 4.8 %copy-start.1 = (f32[40,1280]{1,0:T(8,128)S(1)}, f32[40,1280]{1,0:T(8,128)}, u32[]{:S(2)}) copy-start(f32[40,1280]{1,0:T(8,128)} %param.14) | copy-start | bytes 614404
  1.4 4.6 %copy-start.2 = (f32[40,1280]{1,0:T(8,128)S(1)}, f32[40,1280]{1,0:T(8,128)}, u32[]{:S(2)}) copy-start(f32[40,1280]{1,0:T(8,128)} %param.15) | copy-start | bytes 614404
  4.7 1.8 copy-start.3
  8.3 62.3 %copy-start.11 = (f32[80]{0:T(128)S(1)}, f32[80]{0:T(128)}, u32[]{:S(2)}) copy-start(f32[80]{0:T(128)} %param.24) | copy-start | bytes 964
  184.0 140.0 %copy-start.10 = (f32[8,1280]{1,0:T(8,128)S(1)}, f32[8,1280]{1,0:T(8,128)}, u32[]{:S(2)}) copy-start(f32[8,1280]{1,0:T(8,128)} %get-tuple-element.66) | copy-start | bytes 122884
  325.9 2.6 copy-start
  328.5 1.1 copy-start.9
  328.5 1.8 copy-start.8
  328.5 2.4 copy-start.7
  328.5 3.1 copy-start.6
  329.6 2.7 copy-start.5
  329.6 3.4 %copy-start.4 = (f32[40,1280]{1,0:T(8,128)S(1)}, f32[40,1280]{1,0:T(8,128)}, u32[]{:S(2)}) copy-start(f32[40,1280]{1,0:T(8,128)} %get-tuple-element.97) | copy-start | bytes 614404

commit v2 on v1

--- a/solution.py
+++ b/solution.py
@@ -50,16 +50,14 @@
     )
 
 
-def gather_kernel(S, F, x, wq, sm, wm, x_all, wq_all, sm_all, wm_all, xv, qv, sv, mv, local,
+def gather_kernel(S, F, x, sm, w_q, w_k, w_v, w_o, w_1, w_2, x_all, wq_all, sm_all, wm_all, xv, qv, sv, mv, local,
                   xs, xr, qs, qr, ss, sr, ms, mr):
     s, f, p, c = spots()
     P_ = S // 2
     other = 1 - c
     loads = [
         pltpu.make_async_copy(sm, sv, local.at[0]),
-        pltpu.make_async_copy(wq, qv, local.at[1]),
         pltpu.make_async_copy(x, xv, local.at[2]),
-        pltpu.make_async_copy(wm, mv, local.at[3]),
     ]
     for load in loads:
         load.start()
@@ -93,13 +91,16 @@
     keep0.start()
     for i in range(1, F):
         go(remote(sv, sm_all.at[s, f], ss, sr, i, (s, deep(i))))
-    loads[1].wait()
+    C = qv.shape[2] // 3
+    for n, w in enumerate((w_q, w_k, w_v)):
+        for to in range(S):
+            qv[to, :, n * C : (n + 1) * C] = w[:, to * C : (to + 1) * C].astype(bf)
     keep1 = pltpu.make_async_copy(qv.at[s], wq_all.at[s, f], local.at[1])
     keep1.start()
     for i in range(1, S):
         to = lax.rem(s + i, S)
         go(remote(qv.at[to], wq_all.at[s, f], qs, qr, i, (to, f)))
-    loads[2].wait()
+    loads[1].wait()
     keep2 = pltpu.make_async_copy(xv, x_all.at[s], local.at[2])
     keep2.start()
     if P_ == 4:
@@ -112,7 +113,8 @@
         for i in range(1, P_):
             go(remote(xv, x_all.at[s], xs, xr, i, (chip(i), f)))
     go(remote(xv, x_all.at[s], xs, xr, 0, mate))
-    loads[3].wait()
+    for n, w in enumerate((w_o, w_1, w_2)):
+        mv[n] = w[...].astype(bf)
     keep3 = pltpu.make_async_copy(mv, wm_all.at[:, f], local.at[3])
     keep3.start()
     for i in range(1, F):
@@ -178,13 +180,16 @@
         copy.wait_send()
 
 
-def gather_all(S, F, x, wq, sm, wm):
+def gather_all(S, F, x, sm, *weights):
+    R, D = weights[0].shape
+    C3 = 3 * D // S
+    vm = pl.BlockSpec(memory_space=pltpu.VMEM)
     any_ = pl.BlockSpec(memory_space=pl.ANY)
     shapes = [
         (S,) + x.shape,
-        (S, F) + wq.shape[1:],
+        (S, F, R, C3),
         (S, F) + sm.shape,
-        (wm.shape[0], F) + wm.shape[1:],
+        (3, F, R, D),
     ]
     P_ = S // 2
     dma = pltpu.SemaphoreType.DMA
@@ -195,21 +200,21 @@
     return pl.pallas_call(
         functools.partial(gather_kernel, S, F),
         out_shape=[
-            jax.ShapeDtypeStruct(sh, a.dtype) for sh, a in zip(shapes, (x, wq, sm, wm), strict=True)
+            jax.ShapeDtypeStruct(sh, bf) for sh in shapes
         ],
-        in_specs=[any_] * 4,
+        in_specs=[any_] * 2 + [vm] * 6,
         out_specs=[any_] * 4,
         scratch_shapes=[
             pltpu.VMEM(x.shape, x.dtype),
-            pltpu.VMEM(wq.shape, wq.dtype),
+            pltpu.VMEM((S, R, C3), bf),
             pltpu.VMEM(sm.shape, sm.dtype),
-            pltpu.VMEM(wm.shape, wm.dtype),
+            pltpu.VMEM((3, R, D), bf),
             dma((4,)),
         ]
         + sems,
         compiler_params=pltpu.CompilerParams(collective_id=1, has_side_effects=True),
         name="gather",
-    )(x, wq, sm, wm)
+    )(x, sm, *weights)
 
 
 def xor(a, b, n):
@@ -1395,12 +1400,11 @@
     length = tokens * groups
     shard = w_query.shape[0]
     x_low = inputs.reshape(tokens, width)
-    qkv_rows = jnp.stack([w_query, w_key, w_value], 1).astype(bf).reshape(shard, 3, groups, cols)
-    qkv_rows = qkv_rows.transpose(2, 0, 1, 3).reshape(groups, shard, 3 * cols)
     small = jnp.stack([gain_first, gain_second, bias_up, bias_down], 0)
     small = jnp.pad(small.astype(bf), ((0, 12), (0, 128 - shard)))
-    weights = jnp.stack([w_proj, w_up, w_down], 0).astype(bf)
-    x_all, qkv_w, small, weights = gather_all(groups, rows_of, x_low, qkv_rows, small, weights)
+    x_all, qkv_w, small, weights = gather_all(
+        groups, rows_of, x_low, small, w_query, w_key, w_value, w_proj, w_up, w_down
+    )
     qkv_w = qkv_w.reshape(width, 3 * cols)
     small = small[:, :, :4, :shard].transpose(2, 0, 1, 3).reshape(4, width).astype(f32)
     scale_dims = jax.nn.softplus(query_scale) * log_two_inverse / math.sqrt(HD)

time: 334 us -> 329 us (0.985)
  other arithmetic: 7.6 us -> 3.46 us
    unnamed x32 -> x26, local copies, waits for them, and re-layouts: 7.75 us -> 7.73 us
where the time goes in v2:
time: 329 us
  Pallas kernels  312 us (95%)
  local copies, waits for them, and re-layouts  12 us (4%)
  other arithmetic  3.46 us (1%)
    pallas_call x1, Pallas kernels, backward_all(): pl.pallas_call(functools.partial(backward_kernel, S, F, nh), out_shape=[s...  140 us
    pallas_call x1, Pallas kernels, forward_all(): pl.pallas_call(functools.partial(forward_kernel, S, F, nh), out_shape=[sh...  68.3 us
    pallas_call x1, Pallas kernels, gather_all(): pl.pallas_call(functools.partial(gather_kernel, S, F), out_shape=[jax.Sha...  61.2 us
    pallas_call x1, Pallas kernels, middle_all(): pl.pallas_call(functools.partial(middle_kernel, S, F, nh), out_shape=[sha...  42.8 us
    unnamed x26, local copies, waits for them, and re-layouts  7.73 us

profile of v2, /device:TPU:0, one launch (start us, length us, event | category | flops | bytes accessed | tf_op | source)
XLA Modules:
  0.0 328.6 jit_solution(17281208503784711640)
XLA Ops:
  0.6 0.7 convert_bitcast_fusion.1
  1.3 0.7 convert_bitcast_fusion.3
  2.0 0.6 fusion.8.sm
  2.6 61.2 %gather.1 = (bf16[8,512,1280]{2,1,0:T(8,128)(2,1)}, bf16[8,4,40,480]{3,2,1,0:T(8,128)(2,1)}, bf16[8,4,16,128]{3,2,1,0:T(8,128)(2,1)}, bf16[3,4,40,1280]{3,2,1,0:T(8,128)(2,1)}) custom-call(bf16[512,1280]{1,0:T(8,128)(2,1)} %bitcast.28, bf16[16,128]{1,0:T(8,128)(2,1)} %fusion.8.sm, f32[40,1280]{1,0:T(8,128)} %w_q.1, f32[40,1280]{1,0:T(8,128)} %w_k.1, ...), custom_call_target="tpu_custom_call" | custom-call | tf_op jit(solution)/shard_map/gather/pallas_call | solution.py:200
  63.8 0.9 convert_bitcast_fusion
  64.7 0.7 slice.33.g1
  65.4 0.8 broadcast_in_dim_tile.5.sc
  66.2 68.3 %forward.1 = (bf16[8,512,1280]{2,1,0:T(8,128)(2,1)}, bf16[160,4096]{1,0:T(8,128)(2,1)}, bf16[160,4096]{1,0:T(8,128)(2,1)}, bf16[2,4096,80]{2,1,0:T(8,128)(2,1)},...) custom-call(bf16[8,512,1280]{2,1,0:T(8,128)(2,1)} %get-tuple-element, ...), custom_call_target="tpu_custom_call" | custom-call | tf_op jit(solution)/shard_map/forward/pallas_call | solution.py:491
  134.5 0.7 convert_element_type.12.small
  135.3 42.8 %middle.1 = (bf16[512,1280]{1,0:T(8,128)(2,1)}, f32[512,1280]{1,0:T(8,128)}, bf16[8,160,512]{2,1,0:T(8,128)(2,1)}, bf16[4,3,160,1280]{3,2,1,0:T(8,128)(2,1)}, f32[8,1280]{1,0:T(8,128)}) custom-call(bf16[8,160,512]{2,1,0:T(8,128)(2,1)} %get-tuple-element.44.mixed, bf16[512,1280]{1,0:T(8,128)(2,1)} %bitcast.29, bf16[512,1280]{1,0:T(8,128)(2,1)} %bitcast.31, ...), custom_call_target="tpu_custom_call" | custom-call | tf_op jit(solution)/shard_map/middle/pallas_call | solution.py:735
  178.1 140.1 %backward.1 = (f32[40,1280]{1,0:T(8,128)}, f32[40,1280]{1,0:T(8,128)}, f32[40,1280]{1,0:T(8,128)}, bf16[512,1280]{1,0:T(8,128)(2,1)}, f32[40,1280]{1,0:T(8,128)}...) custom-call(bf16[8,160,512]{2,1,0:T(8,128)(2,1)} %get-tuple-element., ...), custom_call_target="tpu_custom_call" | custom-call | tf_op jit(solution)/shard_map/backward/pallas_call | solution.py:1319
  318.2 0.7 slice.34
  319.0 0.5 slice_bitcast_fusion
  319.5 0.7 slice_reduce_fusion.1
  320.2 0.1 reshape_squeeze.3
  320.3 0.5 fusion.14
  320.8 2.6 copy.38
  323.4 1.1 copy.39
  324.5 0.7 copy.40
  325.2 0.7 copy.41
  325.8 0.7 copy.42
  326.5 0.7 copy.43
  327.2 0.7 copy.44
  327.9 0.7 copy.45
  (25 shorter events, 0.2 us)
Async XLA Ops:
  2.6 62.8 %copy-start.8 = (f32[80]{0:T(128)S(1)}, f32[80]{0:T(128)}, u32[]{:S(2)}) copy-start(f32[80]{0:T(128)} %param.24) | copy-start | bytes 964
  178.1 140.8 %copy-start.7 = (f32[8,1280]{1,0:T(8,128)S(1)}, f32[8,1280]{1,0:T(8,128)}, u32[]{:S(2)}) copy-start(f32[8,1280]{1,0:T(8,128)} %get-tuple-element.66) | copy-start | bytes 122884
  320.8 2.6 copy-start
  323.4 1.1 copy-start.6
  323.4 1.8 copy-start.5
  323.4 2.4 copy-start.4
  323.4 3.1 copy-start.3
  324.5 2.7 copy-start.2
  324.5 3.4 %copy-start.1 = (f32[40,1280]{1,0:T(8,128)S(1)}, f32[40,1280]{1,0:T(8,128)}, u32[]{:S(2)}) copy-start(f32[40,1280]{1,0:T(8,128)} %get-tuple-element.95) | copy-start | bytes 614404

commit v3 on v2

--- a/solution.py
+++ b/solution.py
@@ -526,7 +526,7 @@
 
 
 def middle_kernel(S, F, nh, mixed, x, ct, wm, small, out, dx2, dm, gi, vec,
-                  mx, lt, xv, cv, wv, x2, n2, dn, ab, ub, eb, r2, sb, rb, ob, dov, rv, vz, vp, local, wsem,
+                  mx, lt, xv, cv, wv, x2, n2, dn, ab, ub, eb, r2, sb, rb, ob, dov, et, rv, vz, vp, local, wsem,
                   dsend, drecv, gsend, grecv, vsend, vrecv):
     s, f, p, c = spots()
     P_ = S // 2
@@ -639,17 +639,19 @@
     def head_out(i, to):
         return remote(dov.at[i], dm.at[s], dsend, drecv, i, (to, f))
 
+    et[...] = jnp.transpose(eb[...])
+
     def heads(i, _):
         to = lax.rem(s + i, S)
         rows_of = pl.ds(pl.multiple_of(to * C, C), C)
-        dov[i] = dot(wv[0, rows_of, :], eb[...], 1, 1).astype(bf)
+        dov[i] = dot(wv[0, rows_of, :], et[...]).astype(bf)
 
         head_out(i, to).start()
         return 0
 
     lax.fori_loop(1, S, heads, 0)
     mine = pl.ds(pl.multiple_of(s * C, C), C)
-    dov[0] = dot(wv[0, mine, :], eb[...], 1, 1).astype(bf)
+    dov[0] = dot(wv[0, mine, :], et[...]).astype(bf)
     home = pltpu.make_async_copy(dov.at[0], dm.at[s], local.at[1])
     home.start()
 
@@ -760,6 +762,7 @@
             V((NW, P_ * G, D), bf),
             V((NW, P_ * G, D), bf),
             V((S, C, T), bf),
+            V((D, T), bf),
             V((8, D), f32),
             V((F, 8, D), f32),
             V((S, 8, D), f32),
@@ -779,10 +782,11 @@
     )(mixed, x, ct, wm, small)
 
 
-def backward_kernel(S, F, nh, dm, qt, kt, q, k, v, ot, lse, n1, x_all, w, sc, g1, gi, dx2,
+def backward_kernel(S, F, nh, dm, qt_in, kt_in, q_in, k_in, v_in, ot_in, lse, n1, x_all, w, sc, g1,
+                    gi, dx2,
                     o_proj, o_up, o_down, in_out, o_q, o_k, o_v, vec_out, gp, gr_, gj,
-                    dmt, wt, dwt, fm, tm, nx, xx, rr, mb, own, bi, bp, rl, ga, gb, gz, qi, qo,
-                    vi, vz, vp, gf, gs_, local, nsem, bload,
+                    qt, kt, q, k, v, ot, dmt, wt, dwt, fm, tm, nx, xx, rr, mb, own, bi, bp, rl, ga, gb, gz, qi, qo,
+                    vi, vz, vp, gf, gs_, local, nsem, bload, early,
                     gsend, grecv, bsend, brecv, qsend, qrecv, vsend, vrecv):
     s, f, p, c = spots()
     P_ = S // 2
@@ -821,6 +825,10 @@
         pltpu.make_async_copy(dm.at[b], dmt.at[:, b * T : (b + 1) * T], bload.at[b])
         for b in range(S)
     ]
+    pairs_in = ((qt_in, qt), (kt_in, kt), (q_in, q), (k_in, k), (v_in, v), (ot_in, ot))
+    loads += [
+        pltpu.make_async_copy(src, dst, early.at[n]) for n, (src, dst) in enumerate(pairs_in)
+    ]
     for load in loads:
         load.start()
     greet(S, F)
@@ -830,8 +838,6 @@
     dwt[...] = jnp.zeros_like(dwt)
     gf[...] = jnp.zeros_like(gf)
     gs_[...] = jnp.zeros_like(gs_)
-    for load in loads:
-        load.wait()
 
     def slabs(body):
         def one(n, _):
@@ -890,6 +896,9 @@
     else:
         for i in order[:-1]:
             out_g(i).start()
+
+    for load in loads:
+        load.wait()
 
     rows = 64
     wide = 256 if D % 256 == 0 else D
@@ -1331,9 +1340,15 @@
             shape((2, NW, F // 2, R, D), bf),
             shape((2, NW, F // 2, R, D), bf),
         ],
-        in_specs=[any_] + [vm] * 7 + [any_, any_, vm, vm, vm, any_, any_],
+        in_specs=[any_] * 7 + [vm, any_, any_, vm, vm, vm, any_, any_],
         out_specs=[any_] * 11,
         scratch_shapes=[
+            V((C, L), bf),
+            V((C, L), bf),
+            V((nh, L, HD), bf),
+            V((nh, L, HD), bf),
+            V((nh, L, HD), bf),
+            V((C, L), bf),
             V((C, L), bf),
             V((3 * C, D), bf),
             V((3 * C, D), f32),
@@ -1360,6 +1375,7 @@
             dma((3,)),
             dma((4,)),
             dma((S,)),
+            dma((6,)),
             dma((10 + 2 * P_ + F,)),
             dma((10 + 2 * P_ + F,)),
             dma((max(2 * P_, 10),)),

time: 329 us -> 327 us (level)
  no operation moved by 1% of the time
where the time goes in v3:
time: 327 us
  Pallas kernels  310 us (95%)
  local copies, waits for them, and re-layouts  12 us (4%)
  other arithmetic  3.46 us (1%)
    pallas_call x1, Pallas kernels, backward_all(): pl.pallas_call(functools.partial(backward_kernel, S, F, nh), out_shape=[s...  138 us
    pallas_call x1, Pallas kernels, forward_all(): pl.pallas_call(functools.partial(forward_kernel, S, F, nh), out_shape=[sh...  68.3 us
    pallas_call x1, Pallas kernels, gather_all(): pl.pallas_call(functools.partial(gather_kernel, S, F), out_shape=[jax.Sha...  61.2 us
    pallas_call x1, Pallas kernels, middle_all(): pl.pallas_call(functools.partial(middle_kernel, S, F, nh), out_shape=[sha...  42.8 us
    unnamed x26, local copies, waits for them, and re-layouts  7.73 us

profile of v3, /device:TPU:0, one launch (start us, length us, event | category | flops | bytes accessed | tf_op | source)
XLA Modules:
  0.0 326.6 jit_solution(16471460787910829563)
XLA Ops:
  0.6 0.7 convert_bitcast_fusion.1
  1.3 0.7 convert_bitcast_fusion.3
  2.0 0.6 fusion.8.sm
  2.6 61.2 %gather.1 = (bf16[8,512,1280]{2,1,0:T(8,128)(2,1)}, bf16[8,4,40,480]{3,2,1,0:T(8,128)(2,1)}, bf16[8,4,16,128]{3,2,1,0:T(8,128)(2,1)}, bf16[3,4,40,1280]{3,2,1,0:T(8,128)(2,1)}) custom-call(bf16[512,1280]{1,0:T(8,128)(2,1)} %bitcast.28, bf16[16,128]{1,0:T(8,128)(2,1)} %fusion.8.sm, f32[40,1280]{1,0:T(8,128)} %w_q.1, f32[40,1280]{1,0:T(8,128)} %w_k.1, ...), custom_call_target="tpu_custom_call" | custom-call | tf_op jit(solution)/shard_map/gather/pallas_call | solution.py:200
  63.8 0.9 convert_bitcast_fusion
  64.7 0.7 slice.33.g1
  65.4 0.8 broadcast_in_dim_tile.5.sc
  66.2 68.3 %forward.1 = (bf16[8,512,1280]{2,1,0:T(8,128)(2,1)}, bf16[160,4096]{1,0:T(8,128)(2,1)}, bf16[160,4096]{1,0:T(8,128)(2,1)}, bf16[2,4096,80]{2,1,0:T(8,128)(2,1)},...) custom-call(bf16[8,512,1280]{2,1,0:T(8,128)(2,1)} %get-tuple-element, ...), custom_call_target="tpu_custom_call" | custom-call | tf_op jit(solution)/shard_map/forward/pallas_call | solution.py:491
  134.5 0.7 convert_element_type.12.small
  135.3 42.8 %middle.1 = (bf16[512,1280]{1,0:T(8,128)(2,1)}, f32[512,1280]{1,0:T(8,128)}, bf16[8,160,512]{2,1,0:T(8,128)(2,1)}, bf16[4,3,160,1280]{3,2,1,0:T(8,128)(2,1)}, f32[8,1280]{1,0:T(8,128)}) custom-call(bf16[8,160,512]{2,1,0:T(8,128)(2,1)} %get-tuple-element.44.mixed, bf16[512,1280]{1,0:T(8,128)(2,1)} %bitcast.29, bf16[512,1280]{1,0:T(8,128)(2,1)} %bitcast.31, ...), custom_call_target="tpu_custom_call" | custom-call | tf_op jit(solution)/shard_map/middle/pallas_call | solution.py:737
  178.1 138.1 %backward.1 = (f32[40,1280]{1,0:T(8,128)}, f32[40,1280]{1,0:T(8,128)}, f32[40,1280]{1,0:T(8,128)}, bf16[512,1280]{1,0:T(8,128)(2,1)}, f32[40,1280]{1,0:T(8,128)}...) custom-call(bf16[8,160,512]{2,1,0:T(8,128)(2,1)} %get-tuple-element., ...), custom_call_target="tpu_custom_call" | custom-call | tf_op jit(solution)/shard_map/backward/pallas_call | solution.py:1328
  316.3 0.7 slice.34
  317.1 0.5 slice_bitcast_fusion
  317.6 0.7 slice_reduce_fusion.1
  318.2 0.1 reshape_squeeze.3
  318.4 0.5 fusion.14
  318.9 2.6 copy.38
  321.5 1.1 copy.39
  322.5 0.7 copy.40
  323.2 0.7 copy.41
  323.9 0.7 copy.42
  324.6 0.7 copy.43
  325.3 0.7 copy.44
  326.0 0.7 copy.45
  (25 shorter events, 0.2 us)
Async XLA Ops:
  2.6 62.8 %copy-start.8 = (f32[80]{0:T(128)S(1)}, f32[80]{0:T(128)}, u32[]{:S(2)}) copy-start(f32[80]{0:T(128)} %param.24) | copy-start | bytes 964
  178.1 138.9 %copy-start.7 = (f32[8,1280]{1,0:T(8,128)S(1)}, f32[8,1280]{1,0:T(8,128)}, u32[]{:S(2)}) copy-start(f32[8,1280]{1,0:T(8,128)} %get-tuple-element.66) | copy-start | bytes 122884
  318.9 2.6 copy-start
  321.5 1.1 copy-start.6
  321.5 1.8 copy-start.5
  321.5 2.4 copy-start.4
  321.5 3.1 copy-start.3
  322.5 2.7 copy-start.2
  322.5 3.4 %copy-start.1 = (f32[40,1280]{1,0:T(8,128)S(1)}, f32[40,1280]{1,0:T(8,128)}, u32[]{:S(2)}) copy-start(f32[40,1280]{1,0:T(8,128)} %get-tuple-element.95) | copy-start | bytes 614404

commit v4 on v3

--- a/solution.py
+++ b/solution.py
@@ -235,8 +235,8 @@
     return out
 
 
-def forward_kernel(S, F, nh, x_all, w, g1, sc, wz, n1, qt, kt, qn, kk, vn, ot, lse, mixed, wm,
-                   wt, vt, xb, nb, wv, inx, outn, local, osend, orecv, wsend, wrecv):
+def forward_kernel(S, F, nh, x_all, w, g1, sc, wz, n1, qt_o, kt_o, qn_o, kk_o, vn_o, ot, lse,
+                   mixed, wm, qt, kt, qn, kk, vn, wt, vt, xb, nb, wv, inx, outn, local, late, osend, orecv, wsend, wrecv):
     s, f, p, c = spots()
     P_ = S // 2
     T, D = x_all.shape[1], x_all.shape[2]
@@ -353,6 +353,14 @@
             relay(i).start()
     store(S - 2).wait()
     store(S - 1).wait()
+    kept = [
+        pltpu.make_async_copy(src, dst, late.at[n])
+        for n, (src, dst) in enumerate(
+            ((qt, qt_o), (kt, kt_o), (qn, qn_o), (kk, kk_o), (vn, vn_o))
+        )
+    ]
+    for copy in kept:
+        copy.start()
 
     r = BQ // BK
 
@@ -459,6 +467,8 @@
     last.wait_send()
     own.wait()
     keep.wait()
+    for copy in kept:
+        copy.wait()
     near.wait()
     if square:
         for i in (1, 2):
@@ -503,8 +513,13 @@
             shape((NW, S, F, R, D), bf),
         ],
         in_specs=[any_, vm, vm, vm, any_],
-        out_specs=[any_] + [vm] * 7 + [any_, any_],
+        out_specs=[any_] * 6 + [vm] * 2 + [any_, any_],
         scratch_shapes=[
+            V((C, L), bf),
+            V((C, L), bf),
+            V((nh, L, HD), bf),
+            V((nh, L, HD), bf),
+            V((nh, L, HD), bf),
             V((3 * C, D), bf),
             V((C, L), bf),
             V((2, T, D), bf),
@@ -513,6 +528,7 @@
             dma((2,)),
             dma((2,)),
             dma((2,)),
+            dma((5,)),
             dma((2 * P_,)),
             dma((2 * P_,)),
             dma((max(2 * P_, 12),)),

time: 327 us -> 325 us (level)
  no operation moved by 1% of the time
where the time goes in v4:
time: 325 us
  Pallas kernels  309 us (95%)
  local copies, waits for them, and re-layouts  12 us (4%)
  other arithmetic  3.46 us (1%)
    pallas_call x1, Pallas kernels, backward_all(): pl.pallas_call(functools.partial(backward_kernel, S, F, nh), out_shape=[s...  138 us
    pallas_call x1, Pallas kernels, forward_all(): pl.pallas_call(functools.partial(forward_kernel, S, F, nh), out_shape=[sh...  65.6 us
    pallas_call x1, Pallas kernels, gather_all(): pl.pallas_call(functools.partial(gather_kernel, S, F), out_shape=[jax.Sha...  61.2 us
    pallas_call x1, Pallas kernels, middle_all(): pl.pallas_call(functools.partial(middle_kernel, S, F, nh), out_shape=[sha...  43.8 us
    unnamed x26, local copies, waits for them, and re-layouts  7.73 us

profile of v4, /device:TPU:0, one launch (start us, length us, event | category | flops | bytes accessed | tf_op | source)
XLA Modules:
  0.0 324.7 jit_solution(4640992384737185528)
XLA Ops:
  0.6 0.7 convert_bitcast_fusion.1
  1.3 0.7 convert_bitcast_fusion.3
  2.0 0.6 fusion.8.sm
  2.6 61.2 %gather.1 = (bf16[8,512,1280]{2,1,0:T(8,128)(2,1)}, bf16[8,4,40,480]{3,2,1,0:T(8,128)(2,1)}, bf16[8,4,16,128]{3,2,1,0:T(8,128)(2,1)}, bf16[3,4,40,1280]{3,2,1,0:T(8,128)(2,1)}) custom-call(bf16[512,1280]{1,0:T(8,128)(2,1)} %bitcast.28, bf16[16,128]{1,0:T(8,128)(2,1)} %fusion.8.sm, f32[40,1280]{1,0:T(8,128)} %w_q.1, f32[40,1280]{1,0:T(8,128)} %w_k.1, ...), custom_call_target="tpu_custom_call" | custom-call | tf_op jit(solution)/shard_map/gather/pallas_call | solution.py:200
  63.8 0.9 convert_bitcast_fusion
  64.7 0.7 slice.33.g1
  65.4 0.8 broadcast_in_dim_tile.5.sc
  66.2 65.6 %forward.1 = (bf16[8,512,1280]{2,1,0:T(8,128)(2,1)}, bf16[160,4096]{1,0:T(8,128)(2,1)}, bf16[160,4096]{1,0:T(8,128)(2,1)}, bf16[2,4096,80]{2,1,0:T(8,128)(2,1)},...) custom-call(bf16[8,512,1280]{2,1,0:T(8,128)(2,1)} %get-tuple-element, ...), custom_call_target="tpu_custom_call" | custom-call | tf_op jit(solution)/shard_map/forward/pallas_call | solution.py:501
  131.8 0.7 convert_element_type.12.small
  132.5 43.8 %middle.1 = (bf16[512,1280]{1,0:T(8,128)(2,1)}, f32[512,1280]{1,0:T(8,128)}, bf16[8,160,512]{2,1,0:T(8,128)(2,1)}, bf16[4,3,160,1280]{3,2,1,0:T(8,128)(2,1)}, f32[8,1280]{1,0:T(8,128)}) custom-call(bf16[8,160,512]{2,1,0:T(8,128)(2,1)} %get-tuple-element.44.mixed, bf16[512,1280]{1,0:T(8,128)(2,1)} %bitcast.29, bf16[512,1280]{1,0:T(8,128)(2,1)} %bitcast.31, ...), custom_call_target="tpu_custom_call" | custom-call | tf_op jit(solution)/shard_map/middle/pallas_call | solution.py:753
  176.3 138.0 %backward.1 = (f32[40,1280]{1,0:T(8,128)}, f32[40,1280]{1,0:T(8,128)}, f32[40,1280]{1,0:T(8,128)}, bf16[512,1280]{1,0:T(8,128)(2,1)}, f32[40,1280]{1,0:T(8,128)}...) custom-call(bf16[8,160,512]{2,1,0:T(8,128)(2,1)} %get-tuple-element., ...), custom_call_target="tpu_custom_call" | custom-call | tf_op jit(solution)/shard_map/backward/pallas_call | solution.py:1344
  314.4 0.7 slice.34
  315.2 0.5 slice_bitcast_fusion
  315.7 0.7 slice_reduce_fusion.1
  316.3 0.1 reshape_squeeze.3
  316.5 0.5 fusion.14
  317.0 2.6 copy.38
  319.6 1.1 copy.39
  320.6 0.7 copy.40
  321.3 0.7 copy.41
  322.0 0.7 copy.42
  322.7 0.7 copy.43
  323.4 0.7 copy.44
  324.1 0.7 copy.45
  (25 shorter events, 0.2 us)
Async XLA Ops:
  2.6 62.8 %copy-start.8 = (f32[80]{0:T(128)S(1)}, f32[80]{0:T(128)}, u32[]{:S(2)}) copy-start(f32[80]{0:T(128)} %param.24) | copy-start | bytes 964
  176.3 138.7 %copy-start.7 = (f32[8,1280]{1,0:T(8,128)S(1)}, f32[8,1280]{1,0:T(8,128)}, u32[]{:S(2)}) copy-start(f32[8,1280]{1,0:T(8,128)} %get-tuple-element.66) | copy-start | bytes 122884
  317.0 2.6 copy-start
  319.6 1.1 copy-start.6
  319.6 1.8 copy-start.5
  319.6 2.4 copy-start.4
  319.6 3.1 copy-start.3
  320.6 2.7 copy-start.2
  320.6 3.4 %copy-start.1 = (f32[40,1280]{1,0:T(8,128)S(1)}, f32[40,1280]{1,0:T(8,128)}, u32[]{:S(2)}) copy-start(f32[40,1280]{1,0:T(8,128)} %get-tuple-element.95) | copy-start | bytes 614404
